TPU v7x, 32 devices: a whole 2x2x4 slice. The times are simulated.
32 devices in a mesh: child: 2 (over y), row: 4 (over x, core), col: 4 (over z).
Axes of the slice: x: 2, y: 2, z: 4, core: 2. Of those that a mesh axis runs over, the one named last changes fastest.
Arguments:
- child_blocks: float32 [2, 4096, 4096], P('child', 'row', 'col'), as said below
- child_panels: bfloat16 [2, 4096, 1024], P('child', 'row'), may hold values from -0.1875 to 0.1875
- child_patterns: int32 [2, 16, 16], replicated, may hold values from 0 to 1, as said below
- child_maps: int32 [2, 16], replicated, may hold values from 0 to 23, as said below
- parent_place: int32 [24], replicated, may hold values from 0 to 23, as said below
- parent_front: float32 [6144, 6144], P(('child', 'row'), 'col'), as said below
Outputs:
- factored: float32 [6144, 6144], P(('child', 'row'), 'col')
Inputs may be any that keep to these rules, and one draw needn't show every extreme that they name: `parent_place`: a permutation. The entries of one child are distinct; within each aligned block of 4 entries of one child, the values parent_place[child_maps[c, i]] // 6 are distinct. `child_patterns`: symmetric in its two tile dimensions, with ones on the diagonal. `child_blocks`: each child's block is symmetric. `parent_front`: symmetric; the diagonal entries inside stored tiles (parent_place[0], parent_place[0]) and (parent_place[1], parent_place[1]) lie between 200 and 400.
All inputs are finite; a program needn't handle non-finite values.
Results may differ from a plain program's by a relative error of at most 0.0003.
Values may be sent and summed in bfloat16 or wider, within the bound.
A program may use at most 128 MiB of HBM per device.

v0:
```python
import functools

import jax
import jax.numpy as jnp
from jax import lax
from jax.experimental import pallas as pl
from jax.experimental.pallas import tpu as pltpu
from jax.sharding import Mesh, PartitionSpec as P

TILE = 256
F32 = jnp.float32
BF16 = jnp.bfloat16
META = 16
CODED = TILE + META
FULL = 32767.0
NT = (((1,), (1,)), ((), ()))
NN = (((1,), (0,)), ((), ()))


def dot(a, b, dims):
    return lax.dot_general(a, b, dims, preferred_element_type=F32)


def split(x):
    hi = x.astype(BF16)
    return hi, (x - hi.astype(F32)).astype(BF16)


def tile_call(kernel, grid, tables, operands, in_specs, out_shape, out_spec, name, cost=None, scratch=()):
    return pl.pallas_call(
        kernel,
        grid_spec=pltpu.PrefetchScalarGridSpec(
            num_scalar_prefetch=len(tables), grid=grid, in_specs=in_specs, out_specs=out_spec,
            scratch_shapes=list(scratch),
        ),
        out_shape=out_shape,
        name=name,
        cost_estimate=cost,
    )(*tables, *operands)


def powers(k):
    h = jnp.floor(k * 0.5)
    return jnp.exp2(h), jnp.exp2(k - h)


def encode(x):
    top = jnp.maximum(jnp.max(jnp.abs(x), axis=0, keepdims=True), 1e-37)
    k = jnp.ceil(jnp.log2(top) + 1e-3)
    p, r = powers(-k)
    part = jnp.clip(jnp.ceil(top * p * r * FULL), 1.0, FULL)
    q = jnp.clip(x * p * (r * (FULL * FULL / part)), -FULL, FULL)
    q = jnp.floor(q + 0.5).astype(jnp.int32)
    ids = lax.broadcasted_iota(jnp.int32, (META, TILE), 0)
    meta = jnp.where(ids == 0, k.astype(jnp.int32), jnp.where(ids == 1, part.astype(jnp.int32), 0))
    return q.astype(jnp.int16), meta.astype(jnp.int16)


def decode(code):
    meta = code[TILE:, :].astype(jnp.int32).astype(F32)
    p, r = powers(meta[0:1, :])
    q = code[:TILE, :].astype(jnp.int32).astype(F32)
    return q * (meta[1:2, :] * (1.0 / (FULL * FULL)) * p) * r


def pick_kernel(idx, src, out):
    q, meta = encode(src[...])
    out[0, 0, :TILE, :] = q
    out[0, 0, TILE:, :] = meta


def diag_kernel(t, blk, front, ea, eb, out):
    k = pl.program_id(0) * 2 + pl.program_id(1)
    x = jnp.where(t[4, k] != 0, blk[...], 0.0) + jnp.where(t[5, k] != 0, front[...], 0.0)
    out[...] = x - jnp.where(t[6, k] != 0, dot(ea[...], eb[0], NT), 0.0)


def update_kernel(rows, fac, raw, panel, partner, out, coded):
    f = fac[pl.program_id(0), pl.program_id(1)]
    u = decode(raw[0, 0]) - dot(panel[...], partner[0], NT)
    u = jnp.where(f != 0, u, 0.0)
    out[0] = u
    q, meta = encode(u)
    coded[0, :TILE, :] = q
    coded[0, TILE:, :] = meta


def strip_kernel(t, upd, front, out):
    a, q = pl.program_id(0), pl.program_id(1)
    k = a * pl.num_programs(1) + q
    out[...] = jnp.where(t[2, k] != 0, upd[0], 0.0) + jnp.where(t[4, k] != 0, front[...], 0.0)


def final_kernel(t, front, a0, b0, a1, b1, wr, wc, out, wrh, wrl):
    k = pl.program_id(0) * pl.num_programs(1) + pl.program_id(1)
    panel = t[12, k]

    @pl.when(pl.program_id(1) == 0)
    def _():
        wrh[...], wrl[...] = split(wr[...])

    @pl.when(panel == 0)
    def _():
        wch, wcl = split(wc[...])
        big = dot(wrh[...], wch, NN)
        out[...] = front[...] - (big + (dot(wrh[...], wcl, NN) + dot(wrl[...], wch, NN)))
        for m, src in enumerate((a0, b0, a1, b1)):

            @pl.when(t[8 + m, k] != 0)
            def _(src=src):
                out[...] = out[...] + decode(src[0])

    @pl.when(panel == 1)
    def _():
        out[...] = wr[:, :TILE]

    @pl.when(panel == 2)
    def _():
        out[...] = wr[:, TILE:]


BASE = 128
FACTOR_WORK = 40_000_000_000
WIDE = 2


def base_inverse(a_ref, d_ref, x_ref):
    n, step = a_ref.shape[0], 8
    ids = lax.broadcasted_iota(jnp.int32, (step, n), 0)
    lanes = lax.broadcasted_iota(jnp.int32, (step, n), 1)
    a = [a_ref[i * step : (i + 1) * step, :] for i in range(n // step)]
    x = [(lanes == ids + i * step).astype(F32) for i in range(n // step)]
    for j in range(0, n, WIDE):
        c0 = j // step
        chunks = range(c0, n // step)
        cols = [[jnp.broadcast_to(a[i][:, j + t : j + t + 1], (step, n)) for i in chunks] for t in range(WIDE)]
        at = [j + t - c0 * step for t in range(WIDE)]
        rows = [a[c0][p : p + 1, :] for p in at]
        xrows = [x[c0][p : p + 1, :] for p in at]
        for t in range(WIDE):
            pivot = cols[t][0][at[t] : at[t] + 1, :]
            d_ref[j + t : j + t + 1, :] = pivot
            inv = 1.0 / pivot
            low = [c * inv for c in cols[t]]
            low[0] = jnp.where(ids > at[t], low[0], 0.0)
            for s in range(t + 1, WIDE):
                f = cols[t][0][at[s] : at[s] + 1, :]
                g = f * inv
                cols[s] = [c - l * f for c, l in zip(cols[s], low)]
                rows[s] = rows[s] - g * rows[t]
                xrows[s] = xrows[s] - g * xrows[t]
            for n_, i in enumerate(chunks):
                a[i] = a[i] - low[n_] * rows[t]
                x[i] = x[i] - low[n_] * xrows[t]
    for i in range(n // step):
        x_ref[i * step : (i + 1) * step, :] = x[i] * (1.0 / jnp.sqrt(d_ref[i * step : (i + 1) * step, :]))


def factor_kernel(a_in, y, a, blk, piv, inv):
    n = a.shape[0]
    high = functools.partial(lax.dot_general, precision=lax.Precision.HIGHEST, preferred_element_type=F32)
    ids = lax.broadcasted_iota(jnp.int32, (n, n), 0)
    a[...] = a_in[...]
    y[...] = (ids == lax.broadcasted_iota(jnp.int32, (n, n), 1)).astype(F32)

    def one(k, carry):
        at = pl.ds(pl.multiple_of(k * BASE, BASE), BASE)
        blk[...] = a[at, at]
        base_inverse(blk, piv, inv)
        low = high(a[:, at], inv[...], NT)
        low = jnp.where(ids[:, :BASE] >= (k + 1) * BASE, low, 0.0)
        yk = high(inv[...], y[at, :], (((1,), (0,)), ((), ())))
        a[...] = a[...] - high(low, low, NT)
        y[...] = y[...] - high(low, yk, (((1,), (0,)), ((), ())))
        y[at, :] = yk
        return carry

    lax.fori_loop(0, n // BASE, one, 0)


def factor_inverse(d):
    n = d.shape[0]
    return pl.pallas_call(
        factor_kernel,
        out_shape=jax.ShapeDtypeStruct(d.shape, F32),
        scratch_shapes=[pltpu.VMEM((n, n), F32)] + [pltpu.VMEM((BASE, BASE), F32)] * 3,
        name="factor",
        cost_estimate=pl.CostEstimate(flops=FACTOR_WORK, bytes_accessed=8 * n * n, transcendentals=0),
    )(d)


def body(child_blocks, child_panels, child_patterns, child_maps, parent_place, parent_front):
    ci = lax.axis_index("child")
    rx = lax.axis_index("rx")
    core = lax.axis_index("core")
    col = lax.axis_index("col")
    cores = lax.axis_size("core")
    rxn = lax.axis_size("rx")
    row = rx * cores + core
    rown = rxn * cores
    chips = lax.axis_size("child") * rxn
    chip = ci * rxn + rx
    group = ci * rown + row
    block = child_blocks[0]
    own = child_panels[0]
    depth = own.shape[1]
    width = block.shape[0]
    td = width // TILE
    blocks = child_maps.shape[1] // td
    rd = parent_front.shape[0] // TILE
    cd = parent_front.shape[1] // TILE
    slots_n = parent_place.shape[0]
    i32 = jnp.int32

    slots = jnp.sum(
        jnp.where(child_maps[:, :, None] == jnp.arange(slots_n, dtype=i32), parent_place, 0), axis=2
    )
    tiles = jnp.arange(child_maps.shape[1], dtype=i32)
    hit = slots[:, None, :] == jnp.arange(slots_n, dtype=i32)[None, :, None]
    inv = jnp.sum(jnp.where(hit, tiles + 1, 0), axis=2) - 1
    mine = lax.dynamic_index_in_dim(slots, ci, 0, keepdims=False).reshape(blocks, td)
    inv_own = lax.dynamic_index_in_dim(inv, ci, 0, keepdims=False)
    pat = lax.dynamic_index_in_dim(child_patterns, ci, 0, keepdims=False)
    m = (mine // cd)[:, None, :] == jnp.arange(chips, dtype=i32)[None, :, None]
    which = jnp.sum(jnp.where(m, jnp.arange(td, dtype=i32), 0), axis=2)
    there = jnp.any(m, axis=2).astype(i32)
    row_tile = lax.dynamic_index_in_dim(which, row, 0, keepdims=False)
    row_ok = lax.dynamic_index_in_dim(there, row, 0, keepdims=False)
    out_tile = lax.dynamic_index_in_dim(which, col, 0, keepdims=False)
    in_tile = lax.dynamic_index_in_dim(which, col, 1, keepdims=False)
    in_ok = lax.dynamic_index_in_dim(there, col, 1, keepdims=False)
    e = parent_place[:2]
    ie = inv_own[e]

    outgoing = tile_call(
        pick_kernel, (blocks, td), (out_tile,), (block,),
        [pl.BlockSpec((TILE, TILE), lambda z, r, i: (r, i[z]))],
        jax.ShapeDtypeStruct((blocks, td, CODED, TILE), jnp.int16),
        pl.BlockSpec((1, 1, CODED, TILE), lambda z, r, i: (z, r, 0, 0)), "pick",
    )
    raw = lax.all_to_all(outgoing, "col", split_axis=0, concat_axis=0, tiled=True)

    part = lax.dynamic_slice(own, (row_tile[col] * TILE, 0), (TILE, depth))
    part = jnp.where(row_ok[col] != 0, part, jnp.zeros_like(part))

    e_here = jnp.logical_and(ie >= 0, ie // td == row)
    partner = lax.all_gather(part, ("rx", "core"), axis=0)
    pair_a = jnp.array([0, 0, 1, 1], i32)
    pair_b = jnp.array([0, 1, 0, 1], i32)
    ia, ib, ea, eb = ie[pair_a], ie[pair_b], e[pair_a], e[pair_b]
    live = (ia >= 0) & (ib >= 0) & (pat[jnp.maximum(ia, 0), jnp.maximum(ib, 0)] != 0)
    table = jnp.stack([
        jnp.maximum(ia, 0) % td, jnp.maximum(ib, 0) % td, ea % rd, eb % cd,
        live & (ia // td == row) & (ib // td == col),
        (ea // rd == group) & (eb // cd == col),
        live & (ia // td == row) & (eb // cd == col), jnp.maximum(ib, 0) // td,
    ]).astype(i32)
    diag_part = tile_call(
        diag_kernel, (2, 2), (table,), (block, parent_front, own, partner),
        [
            pl.BlockSpec((TILE, TILE), lambda a, b, t: (t[0, a * 2 + b], t[1, a * 2 + b])),
            pl.BlockSpec((TILE, TILE), lambda a, b, t: (t[2, a * 2 + b], t[3, a * 2 + b])),
            pl.BlockSpec((TILE, depth), lambda a, b, t: (t[0, a * 2 + b], 0)),
            pl.BlockSpec((1, TILE, depth), lambda a, b, t: (t[7, a * 2 + b], 0, 0)),
        ],
        jax.ShapeDtypeStruct((2 * TILE, 2 * TILE), F32),
        pl.BlockSpec((TILE, TILE), lambda a, b, t: (a, b)), "diag",
    )
    plane = ("child", "rx", "core")
    every = ("child", "rx", "core", "col")
    devices = lax.axis_size(every)
    diagonal = diag_part.reshape(devices, 2 * TILE // devices, 2 * TILE)
    diagonal = lax.all_to_all(diagonal, every, split_axis=0, concat_axis=0, tiled=True)
    diagonal = lax.all_gather(jnp.sum(diagonal, axis=0), every, axis=0, tiled=True)
    diagonal, partner = lax.optimization_barrier((diagonal, partner))
    inverse = factor_inverse(diagonal)

    col_ids = jnp.arange(blocks, dtype=i32) * td + in_tile
    factors = pat[row * td + row_tile][:, col_ids] * row_ok[:, None] * in_ok[None, :]
    update, coded = tile_call(
        update_kernel, (chips, blocks), (row_tile, factors), (raw, own, partner),
        [
            pl.BlockSpec((1, 1, CODED, TILE), lambda p, b, r, f: (b, r[p], 0, 0)),
            pl.BlockSpec((TILE, depth), lambda p, b, r, f: (r[p], 0)),
            pl.BlockSpec((1, TILE, depth), lambda p, b, r, f: (b, 0, 0)),
        ],
        [
            jax.ShapeDtypeStruct((chips, TILE, blocks * TILE), F32),
            jax.ShapeDtypeStruct((chips, CODED, blocks * TILE), jnp.int16),
        ],
        [
            pl.BlockSpec((1, TILE, TILE), lambda p, b, r, f: (p, 0, b)),
            pl.BlockSpec((1, CODED, TILE), lambda p, b, r, f: (p, 0, b)),
        ], "update",
    )
    first = lax.all_to_all(coded, ("child", "rx"), split_axis=0, concat_axis=0, tiled=True)
    second = lax.ppermute(first, "core", [(k, (k + 1) % 2) for k in range(2)])

    my_cols = lax.dynamic_slice_in_dim(inv, col * cd, cd, 1)
    my_rows = lax.dynamic_slice_in_dim(inv, group * rd, rd, 1)
    cols_own = lax.dynamic_index_in_dim(my_cols, ci, 0, keepdims=False)
    grid_q = jnp.broadcast_to(jnp.arange(cd, dtype=i32), (2, cd))
    e2 = jnp.broadcast_to(e[:, None], (2, cd))
    cols2 = jnp.broadcast_to(cols_own[None, :], (2, cd))
    table = jnp.stack([
        e2 // cd, jnp.maximum(cols2, 0) // td,
        (e_here[:, None] & (cols2 >= 0)),
        e2 % rd, (e2 // rd == group),
    ]).astype(i32).reshape(5, 2 * cd)
    strip_part = tile_call(
        strip_kernel, (2, cd), (table,), (update, parent_front),
        [
            pl.BlockSpec((1, TILE, TILE), lambda a, q, t: (t[0, a * cd + q], 0, t[1, a * cd + q])),
            pl.BlockSpec((TILE, TILE), lambda a, q, t: (t[3, a * cd + q], q)),
        ],
        jax.ShapeDtypeStruct((2 * TILE, cd * TILE), F32),
        pl.BlockSpec((TILE, TILE), lambda a, q, t: (a, q)), "strip",
    )
    piece = lax.psum_scatter(strip_part, plane, scatter_dimension=0, tiled=True)
    pieces = jnp.broadcast_to(piece[None], (blocks,) + piece.shape)
    pieces = lax.all_to_all(pieces, "col", split_axis=0, concat_axis=0, tiled=True)
    strip = lax.all_gather(piece, plane, axis=0, tiled=True)
    pieces = pieces.reshape(chips, piece.shape[0], cores, rd * TILE).transpose(0, 2, 1, 3)
    pieces = pieces.reshape(chips * cores, piece.shape[0], rd * TILE)
    half = lax.all_to_all(pieces, plane, split_axis=0, concat_axis=0, tiled=True)
    half = half.reshape(2 * TILE, rd * TILE)
    wc = lax.dot_general(inverse, strip, (((1,), (0,)), ((), ())), precision=lax.Precision.HIGHEST)
    wr = lax.dot_general(half, inverse, (((0,), (1,)), ((), ())), precision=lax.Precision.HIGHEST)

    rr = jnp.broadcast_to(my_rows[:, :, None], (2, rd, cd))
    cc = jnp.broadcast_to(my_cols[:, None, :], (2, rd, cd))
    ok = (rr >= 0) & (cc >= 0)
    send_row = jnp.maximum(rr, 0) // td
    same = send_row % cores == core
    send = jnp.arange(2, dtype=i32)[:, None, None] * rxn + send_row // cores
    from_b = jnp.maximum(cc, 0) // td
    lists = []
    for c in range(2):
        for kind in (same, ~same):
            flag = ok[c] & kind[c]
            lists.append((jnp.where(flag, send[c], 0), jnp.where(flag, from_b[c], 0), flag.astype(i32)))
    here = col * cd + jnp.arange(cd, dtype=i32)
    panel = jnp.where(here == e[0], 1, jnp.where(here == e[1], 2, 0))
    rows = [x[n] for n in (0, 1) for x in lists] + [x[2] for x in lists]
    rows.append(jnp.broadcast_to(panel, (rd, cd)))
    table = jnp.stack(rows).reshape(13, rd * cd)

    def from_list(n):
        return pl.BlockSpec(
            (1, CODED, TILE), lambda i, j, t: (t[n, i * cd + j], 0, t[4 + n, i * cd + j])
        )

    return tile_call(
        final_kernel, (rd, cd), (table,), (parent_front, first, second, first, second, wr, wc),
        [pl.BlockSpec((TILE, TILE), lambda i, j, t: (i, j))] + [from_list(n) for n in range(4)] + [
            pl.BlockSpec((TILE, 2 * TILE), lambda i, j, t: (i, 0)),
            pl.BlockSpec((2 * TILE, TILE), lambda i, j, t: (0, j)),
        ],
        jax.ShapeDtypeStruct(parent_front.shape, F32),
        pl.BlockSpec((TILE, TILE), lambda i, j, t: (i, j)), "final",
        scratch=[pltpu.VMEM((TILE, 2 * TILE), BF16)] * 2,
    )


def solution(mesh):
    child, row, col = mesh.devices.shape
    cores = child * row // col
    fine = Mesh(mesh.devices.reshape(child, row // cores, cores, col), ("child", "rx", "core", "col"))
    return jax.shard_map(
        body,
        mesh=fine,
        in_specs=(
            P("child", ("rx", "core"), "col"),
            P("child", ("rx", "core"), None),
            P(),
            P(),
            P(),
            P(("child", "rx", "core"), "col"),
        ),
        out_specs=P(("child", "rx", "core"), "col"),
        check_vma=False,
    )
```

profile of v0, /device:TPU:25, one launch (start us, length us, event | category | flops | bytes accessed | tf_op | source)
XLA Modules:
  0.0 369.4 jit_solution(13020529518859001488)
XLA Ops:
  6.5 0.9 select_reduce_fusion.1
  10.4 1.9 dynamic-slice_select_fusion
  12.4 0.7 pad_clamp_fusion.1
  13.0 0.7 broadcast_add_fusion.5
  14.3 0.7 pad_clamp_fusion
  19.0 17.4 %all-gather.4.cloned.1.call-done.eb.partner = bf16[4,256,1024]{2,1,0:T(8,128)(2,1)} async-done(((bf16[1,256,1024]{2,1,0:T(8,128)(2,1)}), bf16[4,256,1024]{2,1,0:T(8,128)(2,1)}) %all-gather.4.cloned.1.call-update) | async-done | bytes 2097168 | tf_op jit(solution)/shard_map/all_gather | solution.py:247
  36.5 5.6 %diag.1 = f32[512,512]{1,0:T(8,128)} custom-call(s32[8,4]{1,0:T(8,128)} %stack.90.t, f32[1024,1024]{1,0:T(8,128)} %bitcast.128, f32[768,1536]{1,0:T(8,128)} %front.5, bf16[1024,1024]{1,0:T(8,128)(2,1)} %bitcast.130, bf16[4,256,1024]{2,1,0:T(8,128)(2,1)} %all-gather.4.cloned.1.call-done.eb.partner), custom_call_target="tpu_custom_call" | custom-call | tf_op jit(solution)/shard_map/diag/pallas_call | solution.py:30
  42.0 4.8 %all-to-all-start.1 = ((f32[32,16,512]{2,1,0:T(8,128)}), f32[32,16,512]{2,1,0:T(8,128)S(1)}, u32[]{:S(2)}, u32[]{:S(2)}) async-start(f32[32,16,512]{2,1,0:T(8,128)} %bitcast.133), calls=%async_computation.1 | async-start | bytes 2097152 | tf_op jit(solution)/shard_map/all_to_all | solution.py:273
  47.4 11.1 %pick.1 = s16[4,4,272,256]{3,2,1,0:T(8,128)(2,1)} custom-call(s32[4]{0:T(128)} %get-tuple-element.39.idx, f32[1024,1024]{1,0:T(8,128)} %bitcast.129), custom_call_target="tpu_custom_call" | custom-call | tf_op jit(solution)/shard_map/pick/pallas_call | solution.py:30
  58.5 11.8 %all-to-all-done.1 = f32[32,16,512]{2,1,0:T(8,128)S(1)} async-done(((f32[32,16,512]{2,1,0:T(8,128)}), f32[32,16,512]{2,1,0:T(8,128)S(1)}, u32[]{:S(2)}, u32[]{:S(2)}) %all-to-all-start.1) | async-done | bytes 1048608 | tf_op jit(solution)/shard_map/all_to_all | solution.py:273
  70.3 6.5 %all-to-all-start = ((s16[4,4,272,256]{3,2,1,0:T(8,128)(2,1)}), s16[4,4,272,256]{3,2,1,0:T(8,128)(2,1)S(1)}, u32[]{:S(2)}, u32[]{:S(2)}) async-start(s16[4,4,272,256]{3,2,1,0:T(8,128)(2,1)} %pick.1), calls=%async_computation | async-start | bytes 4456448 | tf_op jit(solution)/shard_map/all_to_all | solution.py:241
  77.5 1.2 compare_select_fusion.4
  78.7 0.7 reduce_sum.39
  82.7 0.6 multiply_bitcast_fusion.fac
  83.4 69.2 %all-gather.6.cloned.1.call-done.a_in = f32[512,512]{1,0:T(8,128)} async-done(((f32[16,512]{1,0:T(8,128)}), f32[512,512]{1,0:T(8,128)}) %all-gather.6.cloned.1.call-update) | async-done | bytes 1048592 | tf_op jit(solution)/shard_map/all_gather | solution.py:274
  152.6 1.4 copy-done.2
  154.0 15.5 %update.1 = (f32[4,256,1024]{2,1,0:T(8,128)}, s16[4,272,1024]{2,1,0:T(8,128)(2,1)}) custom-call(s32[4]{0:T(128)} %get-tuple-element.41.rows, s32[4,4]{1,0:T(4,128)} %multiply_bitcast_fusion.fac, s16[4,4,272,256]{3,2,1,0:T(8,128)(2,1)} %copy-done.2, bf16[1024,1024]{1,0:T(8,128)(2,1)} %bitcast.131, bf16[4,256,1024]{2,1,0:T(8,128)(2,1)} %all-gather.4.cloned.1.call-done.eb.partner), custom_call_target="tpu_custom_call" | custom-call | tf_op jit(solution)/shard_map/update/pallas_call | solution.py:30
  169.5 9.4 %strip.1 = f32[512,1536]{1,0:T(8,128)} custom-call(s32[5,12]{1,0:T(8,128)} %stack.91.t, f32[4,256,1024]{2,1,0:T(8,128)} %get-tuple-element.11.upd, f32[768,1536]{1,0:T(8,128)} %front.5), custom_call_target="tpu_custom_call" | custom-call | tf_op jit(solution)/shard_map/strip/pallas_call | solution.py:30
  179.0 35.8 %all_to_all.25.a0.a1 = s16[4,272,1024]{2,1,0:T(8,128)(2,1)S(1)} all-to-all(s16[4,272,1024]{2,1,0:T(8,128)(2,1)} %get-tuple-element.10), channel_id=1, replica_groups=mesh['child'=2,'rx'=2,'core'=2,'col'=4] {'child','rx'}, dimensions={0} | all-to-all | bytes 4456448 | tf_op jit(solution)/shard_map/all_to_all | solution.py:296
  214.8 16.7 %reduce-scatter.2.cloned.1.call-done = f32[64,1536]{1,0:T(8,128)} async-done(((f32[512,1536]{1,0:T(8,128)}), f32[64,1536]{1,0:T(8,128)}) %reduce-scatter.2.cloned.1.call-update) | async-done | bytes 393232 | tf_op jit(solution)/shard_map/reduce_scatter | solution.py:319
  231.4 2.3 broadcast_in_dim.184
  233.8 4.5 %all-to-all-start.3 = ((f32[4,64,1536]{2,1,0:T(8,128)}), f32[4,64,1536]{2,1,0:T(8,128)}, u32[]{:S(2)}, u32[]{:S(2)}) async-start(f32[4,64,1536]{2,1,0:T(8,128)} %broadcast_in_dim.184), calls=%async_computation.4 | async-start | bytes 3145728 | tf_op jit(solution)/shard_map/all_to_all | solution.py:321
  240.0 1.2 stack.89.t
  241.2 1.4 collective-permute-start
  242.6 29.7 %all-to-all-done.3 = f32[4,64,1536]{2,1,0:T(8,128)} async-done(((f32[4,64,1536]{2,1,0:T(8,128)}), f32[4,64,1536]{2,1,0:T(8,128)}, u32[]{:S(2)}, u32[]{:S(2)}) %all-to-all-start.3) | async-done | bytes 1572896 | tf_op jit(solution)/shard_map/all_to_all | solution.py:321
  272.3 1.5 fusion.24
  273.8 1.3 pad_maximum_fusion
  275.0 6.1 %all-to-all-start.4 = ((f32[8,64,768]{2,1,0:T(8,128)}), f32[8,64,768]{2,1,0:T(8,128)}, u32[]{:S(2)}, u32[]{:S(2)}) async-start(f32[8,64,768]{2,1,0:T(8,128)} %bitcast.132), calls=%async_computation.5 | async-start | bytes 3145728 | tf_op jit(solution)/shard_map/all_to_all | solution.py:325
  281.2 46.0 %factor.1 = f32[512,512]{1,0:T(8,128)} custom-call(f32[512,512]{1,0:T(8,128)} %all-gather.6.cloned.1.call-done.a_in), custom_call_target="tpu_custom_call" | custom-call | flops 40000000000 | bytes 2097152 | tf_op jit(solution)/shard_map/factor/pallas_call | solution.py:183
  327.2 8.0 %fusion.26.wr = f32[768,512]{1,0:T(8,128)} fusion(f32[512,768]{1,0:T(8,128)} %bitcast.27, f32[512,512]{1,0:T(8,128)} %factor.1), kind=kOutput, calls=%fused_computation.147 | convolution fusion | flops 2415919104 | bytes 4194304 | tf_op jit(solution)/shard_map/dot_general | solution.py:328
  335.2 8.3 %fusion.27.wc = f32[512,1536]{1,0:T(8,128)} fusion(f32[512,512]{1,0:T(8,128)S(1)} %copy-done.3, f32[512,1536]{1,0:T(8,128)} %all-gather.8.cloned.1.call-done), kind=kOutput, calls=%fused_computation.148 | convolution fusion | flops 4831838208 | bytes 7340032 | tf_op jit(solution)/shard_map/dot_general | solution.py:327
  343.5 19.3 %final.1 = f32[768,1536]{1,0:T(8,128)} custom-call(s32[13,18]{1,0:T(8,128)} %stack.89.t, f32[768,1536]{1,0:T(8,128)} %front.5, s16[4,272,1024]{2,1,0:T(8,128)(2,1)} %copy-done.1, s16[4,272,1024]{2,1,0:T(8,128)(2,1)} %collective-permute-done.b0.b1, s16[4,272,1024]{2,1,0:T(8,128)(2,1)} %copy-done.1, s16[4,272,1024]{2,1,0:T(8,128)(2,1)} %collective-permute-done.b0.b1, ...), custom_call_target="tpu_custom_call" | custom-call | tf_op jit(solution)/shard_map/final/pallas_call | solution.py:30
  (104 shorter events, 12.5 us)
Async XLA Ops:
  6.5 11.1 %copy-start = (s32[2,16,16]{2,1,0:T(8,128)S(1)}, s32[2,16,16]{2,1,0:T(8,128)}, u32[]{:S(2)}) copy-start(s32[2,16,16]{2,1,0:T(8,128)} %param.10) | copy-start | bytes 6148
  6.5 29.9 %all-gather.4.cloned.1.call-start = ((), (), s32[]{:S(2)}) async-start(), calls=%async_computation.6 | async-start | bytes 2621440 | tf_op jit(solution)/shard_map/all_gather | solution.py:247
  42.0 28.3 %all-to-all-start.1 = ((f32[32,16,512]{2,1,0:T(8,128)}), f32[32,16,512]{2,1,0:T(8,128)S(1)}, u32[]{:S(2)}, u32[]{:S(2)}) async-start(f32[32,16,512]{2,1,0:T(8,128)} %bitcast.133), calls=%async_computation.1 | async-start | bytes 2097152 | tf_op jit(solution)/shard_map/all_to_all | solution.py:273
  58.5 18.4 %copy-start.4 = (s32[24]{0:T(128)S(1)}, s32[24]{0:T(128)}, u32[]{:S(2)}) copy-start(s32[24]{0:T(128)} %param.12) | copy-start | bytes 292
  70.3 82.3 %all-to-all-start = ((s16[4,4,272,256]{3,2,1,0:T(8,128)(2,1)}), s16[4,4,272,256]{3,2,1,0:T(8,128)(2,1)S(1)}, u32[]{:S(2)}, u32[]{:S(2)}) async-start(s16[4,4,272,256]{3,2,1,0:T(8,128)(2,1)} %pick.1), calls=%async_computation | async-start | bytes 4456448 | tf_op jit(solution)/shard_map/all_to_all | solution.py:241
  76.8 75.8 %all-gather.6.cloned.1.call-start = ((), (), s32[]{:S(2)}) async-start(), calls=%async_computation.7 | async-start | bytes 1081344 | tf_op jit(solution)/shard_map/all_gather | solution.py:274
  79.4 152.0 %reduce-scatter.2.cloned.1.call-start = ((), (), s32[]{:S(2)}) async-start(), calls=%async_computation.8 | async-start | bytes 3538944 | tf_op jit(solution)/shard_map/reduce_scatter | solution.py:319
  152.6 1.4 copy-start.2
  214.8 26.4 %copy-start.1 = (s16[4,272,1024]{2,1,0:T(8,128)(2,1)}, s16[4,272,1024]{2,1,0:T(8,128)(2,1)S(1)}, u32[]{:S(2)}) copy-start(s16[4,272,1024]{2,1,0:T(8,128)(2,1)S(1)} %all_to_all.25.a0.a1) | copy-start | bytes 6684676
  233.8 38.5 %all-to-all-start.3 = ((f32[4,64,1536]{2,1,0:T(8,128)}), f32[4,64,1536]{2,1,0:T(8,128)}, u32[]{:S(2)}, u32[]{:S(2)}) async-start(f32[4,64,1536]{2,1,0:T(8,128)} %broadcast_in_dim.184), calls=%async_computation.4 | async-start | bytes 3145728 | tf_op jit(solution)/shard_map/all_to_all | solution.py:321
  238.3 96.9 %all-gather.8.cloned.1.call-start = ((), (), s32[]{:S(2)}) async-start(), calls=%async_computation.9 | async-start | bytes 3538944 | tf_op jit(solution)/shard_map/all_gather | solution.py:322
  241.2 102.3 %collective-permute-start = (s16[4,272,1024]{2,1,0:T(8,128)(2,1)S(1)}, s16[4,272,1024]{2,1,0:T(8,128)(2,1)}, u32[]{:S(2)}, u32[]{:S(2)}) collective-permute-start(s16[4,272,1024]{2,1,0:T(8,128)(2,1)S(1)} %all_to_all.25.a0.a1), channel_id=1, source_target_pairs={{0,4},{4,0},{1,5},{5,1},{2,6},{6,2},{3,7},{7,3},{8,12},{12,8},{9,1... | collective-permute-start | bytes 6684680 | tf_op jit(solution)/shard_map/ppermute | solution.py:297
  275.0 52.2 %all-to-all-start.4 = ((f32[8,64,768]{2,1,0:T(8,128)}), f32[8,64,768]{2,1,0:T(8,128)}, u32[]{:S(2)}, u32[]{:S(2)}) async-start(f32[8,64,768]{2,1,0:T(8,128)} %bitcast.132), calls=%async_computation.5 | async-start | bytes 3145728 | tf_op jit(solution)/shard_map/all_to_all | solution.py:325
  327.2 8.0 %copy-start.3 = (f32[512,512]{1,0:T(8,128)S(1)}, f32[512,512]{1,0:T(8,128)}, u32[]{:S(2)}) copy-start(f32[512,512]{1,0:T(8,128)} %factor.1) | copy-start | bytes 3145732
Sparse Core Ops, SparseCore 0:
  12.5 23.9 all-gather.3
  80.6 71.9 all-gather.5
  179.1 52.3 reduce-scatter.1
  240.7 33.3 all-gather.7
where the time goes:
time: 375 us; the launch traced here: 369 us
  waiting for transfers between devices  145 us (39%)
  Pallas kernels  107 us (29%)
  blocking collectives  35.8 us (10%)
  starting transfers between devices  23.4 us (6%)
  local copies, waits for them, and re-layouts  16.7 us (4%)
  matrix products  16.3 us (4%)
  between operations  14.5 us (4%)
  other arithmetic  10.7 us (3%)
    all_gather x1, waiting for transfers between devices, body(): lax.all_gather(jnp.sum(diagonal, axis=0), every, axis=0, tiled=True)  69.2 us
    pallas_call x5, Pallas kernels, tile_call(): pl.pallas_call(kernel, grid_spec=pltpu.PrefetchScalarGridSpec(num_scalar_...  61 us
    pallas_call x1, Pallas kernels, factor_inverse(): pl.pallas_call(factor_kernel, out_shape=jax.ShapeDtypeStruct(d.shape, F32...  46 us
    all_to_all x1, blocking collectives, body(): lax.all_to_all(coded, ('child', 'rx'), split_axis=0, concat_axis=0, tiled...  35.8 us
    all_to_all x1, waiting for transfers between devices, body(): lax.all_to_all(pieces, 'col', split_axis=0, concat_axis=0, tiled=True)  29.7 us
    all_gather x1, waiting for transfers between devices, body(): partner = lax.all_gather(part, ('rx', 'core'), axis=0)  17.4 us
    reduce_scatter x1, waiting for transfers between devices, body(): piece = lax.psum_scatter(strip_part, plane, scatter_dimension=0, tiled=True)  16.7 us
    all_to_all x1, waiting for transfers between devices, body(): lax.all_to_all(diagonal, every, split_axis=0, concat_axis=0, tiled=True)  11.8 us
  transfers between devices with their start and end apart: 9, of which 5 were waited for; matrix products, arithmetic and copies ran while one was open for 10% of the time, Pallas kernels for 15%

commit v1 on v0

--- a/solution.py
+++ b/solution.py
@@ -51,15 +51,16 @@
     part = jnp.clip(jnp.ceil(top * p * r * FULL), 1.0, FULL)
     q = jnp.clip(x * p * (r * (FULL * FULL / part)), -FULL, FULL)
     q = jnp.floor(q + 0.5).astype(jnp.int32)
-    ids = lax.broadcasted_iota(jnp.int32, (META, TILE), 0)
+    ids = lax.broadcasted_iota(jnp.int32, (META, x.shape[1]), 0)
     meta = jnp.where(ids == 0, k.astype(jnp.int32), jnp.where(ids == 1, part.astype(jnp.int32), 0))
     return q.astype(jnp.int16), meta.astype(jnp.int16)
 
 
 def decode(code):
-    meta = code[TILE:, :].astype(jnp.int32).astype(F32)
+    n = code.shape[0] - META
+    meta = code[n:, :].astype(jnp.int32).astype(F32)
     p, r = powers(meta[0:1, :])
-    q = code[:TILE, :].astype(jnp.int32).astype(F32)
+    q = code[:n, :].astype(jnp.int32).astype(F32)
     return q * (meta[1:2, :] * (1.0 / (FULL * FULL)) * p) * r
 
 
@@ -81,29 +82,58 @@
     u = jnp.where(f != 0, u, 0.0)
     out[0] = u
     q, meta = encode(u)
-    coded[0, :TILE, :] = q
-    coded[0, TILE:, :] = meta
-
-
-def strip_kernel(t, upd, front, out):
+    coded[0, 0, :TILE, :] = q
+    coded[0, 0, TILE:, :] = meta
+
+
+def strip_kernel(t, upd, front, out, g):
     a, q = pl.program_id(0), pl.program_id(1)
-    k = a * pl.num_programs(1) + q
-    out[...] = jnp.where(t[2, k] != 0, upd[0], 0.0) + jnp.where(t[4, k] != 0, front[...], 0.0)
-
-
-def final_kernel(t, front, a0, b0, a1, b1, wr, wc, out, wrh, wrl):
-    k = pl.program_id(0) * pl.num_programs(1) + pl.program_id(1)
+    cd = pl.num_programs(1)
+    k = a * cd + q
+    x = jnp.where(t[2, k] != 0, upd[0], 0.0) + jnp.where(t[4, k] != 0, front[...], 0.0)
+    rows = pl.ds(pl.multiple_of(q * TILE, TILE), TILE)
+    g[rows, pl.ds(pl.multiple_of(a * TILE, TILE), TILE)] = x.T
+
+    @pl.when(jnp.logical_and(a == 1, q == cd - 1))
+    def _():
+        n = out.shape[1] - META
+        for p in range(out.shape[0]):
+            code, meta = encode(g[p * n : (p + 1) * n, :])
+            out[p, :n, :] = code
+            out[p, n:, :] = meta
+
+
+def solve_kernel(parts, inverse, out):
+    g = decode(parts[0])
+    for p in range(1, parts.shape[0]):
+        g = g + decode(parts[p])
+    w = lax.dot_general(g, inverse[...], NT, precision=lax.Precision.HIGHEST, preferred_element_type=F32)
+    n = out.shape[0] - META
+    code, meta = encode(w)
+    out[:n, :] = code
+    out[n:, :] = meta
+
+
+def final_kernel(t, front, a0, b0, a1, b1, wr, wc, out, rh, rl, ch, cl):
+    i, j = pl.program_id(0), pl.program_id(1)
+    k = i * pl.num_programs(1) + j
     panel = t[12, k]
 
-    @pl.when(pl.program_id(1) == 0)
+    @pl.when(k == 0)
     def _():
-        wrh[...], wrl[...] = split(wr[...])
+        for src, hi, lo in ((wr, rh, rl), (wc, ch, cl)):
+            n = src.shape[1] - META
+            for p in range(src.shape[0]):
+                at = pl.ds(p * n, n)
+                hi[at, :], lo[at, :] = split(decode(src[p]))
+
+    ri = pl.ds(pl.multiple_of(i * TILE, TILE), TILE)
 
     @pl.when(panel == 0)
     def _():
-        wch, wcl = split(wc[...])
-        big = dot(wrh[...], wch, NN)
-        out[...] = front[...] - (big + (dot(wrh[...], wcl, NN) + dot(wrl[...], wch, NN)))
+        cj = pl.ds(pl.multiple_of(j * TILE, TILE), TILE)
+        big = dot(rh[ri, :], ch[cj, :], NT)
+        out[...] = front[...] - (big + (dot(rh[ri, :], cl[cj, :], NT) + dot(rl[ri, :], ch[cj, :], NT)))
         for m, src in enumerate((a0, b0, a1, b1)):
 
             @pl.when(t[8 + m, k] != 0)
@@ -112,16 +142,249 @@
 
     @pl.when(panel == 1)
     def _():
-        out[...] = wr[:, :TILE]
+        out[...] = rh[ri, :TILE].astype(F32) + rl[ri, :TILE].astype(F32)
 
     @pl.when(panel == 2)
     def _():
-        out[...] = wr[:, TILE:]
+        out[...] = rh[ri, TILE:].astype(F32) + rl[ri, TILE:].astype(F32)
+
+
+MESH = pl.DeviceIdType.MESH
+
+
+class Spot:
+    def __init__(self):
+        self.ci, self.rx = lax.axis_index("child"), lax.axis_index("rx")
+        self.core, self.col = lax.axis_index("core"), lax.axis_index("col")
+        self.rxn, self.cores, self.cols = lax.axis_size("rx"), lax.axis_size("core"), lax.axis_size("col")
+        self.chips = lax.axis_size("child") * self.rxn
+        self.chip = self.ci * self.rxn + self.rx
+        self.other = {"core": 1 - self.core}
+
+    def id(self, chip, core=None):
+        core = self.core if core is None else core
+        return {"child": chip // self.rxn, "rx": lax.rem(chip, self.rxn), "core": core}
+
+    def turn(self, at, d, n):
+        return lax.rem(at + (d % n), n)
+
+
+def greet(ids):
+    bar = pltpu.get_barrier_semaphore()
+    for i in ids:
+        pl.semaphore_signal(bar, inc=1, device_id=i, device_id_type=MESH)
+    pl.semaphore_wait(bar, len(ids))
+
+
+def push(src, dst, send, recv, to):
+    cp = pltpu.make_async_remote_copy(
+        src_ref=src, dst_ref=dst, send_sem=send, recv_sem=recv, device_id=to, device_id_type=MESH
+    )
+    cp.start()
+    return cp
+
+
+def remote_call(kernel, operands, out_shape, out_specs, scratch, cid, name, flops=0):
+    return pl.pallas_call(
+        kernel,
+        out_shape=out_shape,
+        in_specs=[pl.BlockSpec(memory_space=pltpu.VMEM)] * len(operands),
+        out_specs=out_specs,
+        scratch_shapes=scratch,
+        compiler_params=pltpu.CompilerParams(collective_id=cid, has_side_effects=True),
+        cost_estimate=pl.CostEstimate(flops=flops, bytes_accessed=1 << 20, transcendentals=0),
+        name=name,
+    )(*operands)
+
+
+ANY = pl.BlockSpec(memory_space=pl.ANY)
+IN_VMEM = pl.BlockSpec(memory_space=pltpu.VMEM)
+
+
+def panel_kernel(x, out, loc, ss, rs, fs, fr):
+    s = Spot()
+    n = s.rxn
+    me = s.rx * s.cores + s.core
+    peers = [{"rx": s.turn(s.rx, d, n)} for d in range(1, n)]
+    greet(peers + [s.other])
+    keep = pltpu.make_async_copy(x, out.at[me], loc)
+    keep.start()
+    cps = [push(x, out.at[me], ss.at[d], rs.at[d], to) for d, to in enumerate(peers, 1)]
+    fwd = [push(x, out.at[me], fs.at[0], fr.at[0], s.other)]
+    for d, cp in enumerate(cps, 1):
+        cp.wait_recv()
+        at = s.turn(s.rx, -d, n) * s.cores + s.core
+        fwd.append(push(out.at[at], out.at[at], fs.at[d], fr.at[d], s.other))
+    keep.wait()
+    for cp in cps:
+        cp.wait_send()
+    for cp in fwd:
+        cp.wait()
+
+
+def panel_gather(x):
+    n = lax.axis_size("rx")
+    shape = (n * lax.axis_size("core"),) + x.shape
+    dma = pltpu.SemaphoreType.DMA
+    return remote_call(
+        panel_kernel, (x,), jax.ShapeDtypeStruct(shape, x.dtype), ANY,
+        [dma, dma((n,)), dma((n,)), dma((n,)), dma((n,))], 0, "panels",
+    )
+
+
+def sum_kernel(x, out, half, mine, got, part, zgot, ss0, rs0, ss1, rs1, ss2, rs2, ss3, rs3, ss4, rs4, ss5, rs5):
+    s = Spot()
+    nc, nz = s.chips, s.cols
+    chips = [s.turn(s.chip, d, nc) for d in range(1, nc)]
+    cols = [s.turn(s.col, d, nz) for d in range(1, nz)]
+    greet([s.other] + [s.id(t) for t in chips] + [{"col": t} for t in cols])
+    cp = push(x.at[1 - s.core], half, ss0, rs0, s.other)
+    cp.wait()
+    mine[...] = x[s.core] + half[...]
+    cps = [push(mine.at[t], got.at[d], ss1.at[d], rs1.at[d], s.id(t)) for d, t in enumerate(chips)]
+    for cp in cps:
+        cp.wait()
+    total = mine[s.chip]
+    for d in range(nc - 1):
+        total = total + got[d]
+    part[...] = total
+    cps = [push(part.at[t], zgot.at[d], ss2.at[d], rs2.at[d], {"col": t}) for d, t in enumerate(cols)]
+    for cp in cps:
+        cp.wait()
+    total = part[s.col]
+    for d in range(nz - 1):
+        total = total + zgot[d]
+    out[s.core, s.chip, s.col] = total
+    own = out.at[s.core, s.chip, s.col]
+    cps = [push(own, own, ss3.at[d], rs3.at[d], {"col": t}) for d, t in enumerate(cols)]
+    for cp in cps:
+        cp.wait()
+    own = out.at[s.core, s.chip]
+    cps = [push(own, own, ss4.at[d], rs4.at[d], s.id(t)) for d, t in enumerate(chips)]
+    for cp in cps:
+        cp.wait()
+    own = out.at[s.core]
+    push(own, own, ss5, rs5, s.other).wait()
+
+
+def sum_all(x):
+    n = x.shape[0]
+    nc, nz = lax.axis_size(("child", "rx")), lax.axis_size("col")
+    tail = (n // (2 * nc * nz), n)
+    full = jax.ShapeDtypeStruct((2, nc, nz) + tail, F32)
+    dma = pltpu.SemaphoreType.DMA
+    sems = [dma, dma, dma((nc,)), dma((nc,)), dma((nz,)), dma((nz,)), dma((nz,)), dma((nz,)), dma((nc,)), dma((nc,)), dma, dma]
+    half, part = (nc, nz) + tail, (nz,) + tail
+    vm = [pltpu.VMEM(z, F32) for z in (half, half, (nc - 1,) + part, part, (nz - 1,) + tail)]
+    out = remote_call(sum_kernel, (x.reshape(full.shape),), full, IN_VMEM, vm + sems, 1, "total")
+    return out.reshape(n, n)
+
+
+def scatter_kernel(x, out, loc, ss, rs):
+    s = Spot()
+    n = x.shape[0]
+    me = s.chip * s.cores + s.core
+    peers = [s.turn(me, d, n) for d in range(1, n)]
+    ids = [s.id(t // s.cores, lax.rem(t, s.cores)) for t in peers]
+    greet(ids)
+    keep = pltpu.make_async_copy(x.at[me], out.at[me], loc)
+    keep.start()
+    cps = [push(x.at[t], out.at[me], ss.at[d], rs.at[d], i) for d, (t, i) in enumerate(zip(peers, ids))]
+    keep.wait()
+    for cp in cps:
+        cp.wait()
+
+
+def scatter(x):
+    n = x.shape[0]
+    dma = pltpu.SemaphoreType.DMA
+    return remote_call(
+        scatter_kernel, (x,), jax.ShapeDtypeStruct(x.shape, x.dtype), ANY, [dma, dma((n,)), dma((n,))], 2, "strips"
+    )
+
+
+def spread_kernel(x, wc, wr, zbuf, loc, zs, zr, ps, pr, fs, fr, ws, wx, wl):
+    s = Spot()
+    nc, nz, half = s.chips, s.cols, wr.shape[0]
+    me = s.chip * s.cores + s.core
+    slot = lax.rem(me, half)
+    n = nc * s.cores
+    chips = [s.turn(s.chip, d, nc) for d in range(1, nc)]
+    cols = [s.turn(s.col, d, nz) for d in range(1, nz)]
+    plane = [s.turn(me, d, n) for d in range(1, n)]
+    greet([s.id(t // s.cores, lax.rem(t, s.cores)) for t in plane] + [{"col": t} for t in cols])
+    keep = pltpu.make_async_copy(x, wc.at[me], loc)
+    keep.start()
+    zc = [push(x, zbuf.at[s.col], zs.at[d], zr.at[d], {"col": t}) for d, t in enumerate(cols, 1)]
+    pc = [push(x, wc.at[me], ps.at[d], pr.at[d], s.id(t)) for d, t in enumerate(chips, 1)]
+    fc = [push(x, wc.at[me], fs.at[0], fr.at[0], s.other)]
+
+    def hand(src, z, d):
+        here = jnp.logical_and(z == s.chip, s.ci == s.core)
+
+        @pl.when(here)
+        def _():
+            pltpu.make_async_copy(src, wr.at[slot], wl).start()
+
+        @pl.when(jnp.logical_not(here))
+        def _():
+            push(src, wr.at[slot], ws.at[d], wx.at[slot], s.id(z, s.ci))
+
+    def handed(src, z, d):
+        here = jnp.logical_and(z == s.chip, s.ci == s.core)
+
+        @pl.when(here)
+        def _():
+            pltpu.make_async_copy(src, wr.at[slot], wl).wait()
+
+        @pl.when(jnp.logical_not(here))
+        def _():
+            pltpu.make_async_remote_copy(
+                src_ref=src, dst_ref=wr.at[slot], send_sem=ws.at[d], recv_sem=wx.at[slot],
+                device_id=s.id(z, s.ci), device_id_type=MESH,
+            ).wait_send()
+
+    hand(x, s.col, 0)
+    back = [s.turn(s.col, -d, nz) for d in range(nz)]
+    for d in range(1, max(nz, nc)):
+        if d < nz:
+            zc[d - 1].wait_recv()
+            hand(zbuf.at[back[d]], back[d], d)
+        if d < nc:
+            pc[d - 1].wait_recv()
+            at = s.turn(s.chip, -d, nc) * s.cores + s.core
+            fc.append(push(wc.at[at], wc.at[at], fs.at[d], fr.at[d], s.other))
+    for d in range(nz):
+        handed(x if d == 0 else zbuf.at[back[d]], back[d], d)
+    for j in range(half):
+
+        @pl.when(jnp.logical_or(s.ci != s.core, slot != j))
+        def _(j=j):
+            pltpu.make_async_remote_copy(
+                src_ref=wr.at[j], dst_ref=wr.at[j], send_sem=ws.at[0], recv_sem=wx.at[j],
+                device_id=s.other, device_id_type=MESH,
+            ).wait_recv()
+
+    keep.wait()
+    for cp in zc + pc:
+        cp.wait_send()
+    for cp in fc:
+        cp.wait()
+
+
+def spread(x):
+    nc, nz = lax.axis_size(("child", "rx")), lax.axis_size("col")
+    dma = pltpu.SemaphoreType.DMA
+    sems = [dma] + [dma((nz,))] * 2 + [dma((nc,))] * 4 + [dma((nz,)), dma((nc,)), dma]
+    shapes = [jax.ShapeDtypeStruct((n,) + x.shape, x.dtype) for n in (2 * nc, nc)]
+    return remote_call(
+        spread_kernel, (x,), shapes, [ANY, ANY], [pltpu.VMEM((nz,) + x.shape, x.dtype)] + sems, 3, "spread"
+    )
 
 
 BASE = 128
 FACTOR_WORK = 40_000_000_000
-WIDE = 2
+WIDE = 8
 
 
 def base_inverse(a_ref, d_ref, x_ref):
@@ -238,13 +501,13 @@
         jax.ShapeDtypeStruct((blocks, td, CODED, TILE), jnp.int16),
         pl.BlockSpec((1, 1, CODED, TILE), lambda z, r, i: (z, r, 0, 0)), "pick",
     )
-    raw = lax.all_to_all(outgoing, "col", split_axis=0, concat_axis=0, tiled=True)
-
     part = lax.dynamic_slice(own, (row_tile[col] * TILE, 0), (TILE, depth))
     part = jnp.where(row_ok[col] != 0, part, jnp.zeros_like(part))
 
     e_here = jnp.logical_and(ie >= 0, ie // td == row)
-    partner = lax.all_gather(part, ("rx", "core"), axis=0)
+    part, outgoing = lax.optimization_barrier((part, outgoing))
+    raw = lax.all_to_all(outgoing, "col", split_axis=0, concat_axis=0, tiled=True)
+    partner = panel_gather(part)
     pair_a = jnp.array([0, 0, 1, 1], i32)
     pair_b = jnp.array([0, 1, 0, 1], i32)
     ia, ib, ea, eb = ie[pair_a], ie[pair_b], e[pair_a], e[pair_b]
@@ -267,14 +530,10 @@
         pl.BlockSpec((TILE, TILE), lambda a, b, t: (a, b)), "diag",
     )
     plane = ("child", "rx", "core")
-    every = ("child", "rx", "core", "col")
-    devices = lax.axis_size(every)
-    diagonal = diag_part.reshape(devices, 2 * TILE // devices, 2 * TILE)
-    diagonal = lax.all_to_all(diagonal, every, split_axis=0, concat_axis=0, tiled=True)
-    diagonal = lax.all_gather(jnp.sum(diagonal, axis=0), every, axis=0, tiled=True)
-    diagonal, partner = lax.optimization_barrier((diagonal, partner))
+    diagonal = sum_all(diag_part)
     inverse = factor_inverse(diagonal)
 
+    wide = blocks // cores
     col_ids = jnp.arange(blocks, dtype=i32) * td + in_tile
     factors = pat[row * td + row_tile][:, col_ids] * row_ok[:, None] * in_ok[None, :]
     update, coded = tile_call(
@@ -286,14 +545,15 @@
         ],
         [
             jax.ShapeDtypeStruct((chips, TILE, blocks * TILE), F32),
-            jax.ShapeDtypeStruct((chips, CODED, blocks * TILE), jnp.int16),
+            jax.ShapeDtypeStruct((chips, cores, CODED, wide * TILE), jnp.int16),
         ],
         [
             pl.BlockSpec((1, TILE, TILE), lambda p, b, r, f: (p, 0, b)),
-            pl.BlockSpec((1, CODED, TILE), lambda p, b, r, f: (p, 0, b)),
+            pl.BlockSpec((1, 1, CODED, TILE), lambda p, b, r, f: (p, b // wide, 0, b % wide)),
         ], "update",
     )
-    first = lax.all_to_all(coded, ("child", "rx"), split_axis=0, concat_axis=0, tiled=True)
+    coded = coded.reshape((chips * cores,) + coded.shape[2:])
+    first = lax.all_to_all(coded, plane, split_axis=0, concat_axis=0, tiled=True)
     second = lax.ppermute(first, "core", [(k, (k + 1) % 2) for k in range(2)])
 
     my_cols = lax.dynamic_slice_in_dim(inv, col * cd, cd, 1)
@@ -307,33 +567,30 @@
         (e_here[:, None] & (cols2 >= 0)),
         e2 % rd, (e2 // rd == group),
     ]).astype(i32).reshape(5, 2 * cd)
+    share = cd * TILE // (chips * cores)
     strip_part = tile_call(
         strip_kernel, (2, cd), (table,), (update, parent_front),
         [
             pl.BlockSpec((1, TILE, TILE), lambda a, q, t: (t[0, a * cd + q], 0, t[1, a * cd + q])),
             pl.BlockSpec((TILE, TILE), lambda a, q, t: (t[3, a * cd + q], q)),
         ],
-        jax.ShapeDtypeStruct((2 * TILE, cd * TILE), F32),
-        pl.BlockSpec((TILE, TILE), lambda a, q, t: (a, q)), "strip",
-    )
-    piece = lax.psum_scatter(strip_part, plane, scatter_dimension=0, tiled=True)
-    pieces = jnp.broadcast_to(piece[None], (blocks,) + piece.shape)
-    pieces = lax.all_to_all(pieces, "col", split_axis=0, concat_axis=0, tiled=True)
-    strip = lax.all_gather(piece, plane, axis=0, tiled=True)
-    pieces = pieces.reshape(chips, piece.shape[0], cores, rd * TILE).transpose(0, 2, 1, 3)
-    pieces = pieces.reshape(chips * cores, piece.shape[0], rd * TILE)
-    half = lax.all_to_all(pieces, plane, split_axis=0, concat_axis=0, tiled=True)
-    half = half.reshape(2 * TILE, rd * TILE)
-    wc = lax.dot_general(inverse, strip, (((1,), (0,)), ((), ())), precision=lax.Precision.HIGHEST)
-    wr = lax.dot_general(half, inverse, (((0,), (1,)), ((), ())), precision=lax.Precision.HIGHEST)
+        jax.ShapeDtypeStruct((chips * cores, share + META, 2 * TILE), jnp.int16),
+        pl.BlockSpec((chips * cores, share + META, 2 * TILE), lambda a, q, t: (0, 0, 0)), "strip",
+        scratch=[pltpu.VMEM((cd * TILE, 2 * TILE), F32)],
+    )
+    piece = pl.pallas_call(
+        solve_kernel, out_shape=jax.ShapeDtypeStruct(strip_part.shape[1:], jnp.int16), name="solve"
+    )(scatter(strip_part), inverse)
+    wc, wr = spread(piece)
 
     rr = jnp.broadcast_to(my_rows[:, :, None], (2, rd, cd))
     cc = jnp.broadcast_to(my_cols[:, None, :], (2, rd, cd))
     ok = (rr >= 0) & (cc >= 0)
     send_row = jnp.maximum(rr, 0) // td
-    same = send_row % cores == core
-    send = jnp.arange(2, dtype=i32)[:, None, None] * rxn + send_row // cores
     from_b = jnp.maximum(cc, 0) // td
+    same = from_b // wide == core
+    send = jnp.arange(2, dtype=i32)[:, None, None] * rown + send_row
+    from_b = from_b % wide
     lists = []
     for c in range(2):
         for kind in (same, ~same):
@@ -353,12 +610,12 @@
     return tile_call(
         final_kernel, (rd, cd), (table,), (parent_front, first, second, first, second, wr, wc),
         [pl.BlockSpec((TILE, TILE), lambda i, j, t: (i, j))] + [from_list(n) for n in range(4)] + [
-            pl.BlockSpec((TILE, 2 * TILE), lambda i, j, t: (i, 0)),
-            pl.BlockSpec((2 * TILE, TILE), lambda i, j, t: (0, j)),
+            pl.BlockSpec(wr.shape, lambda i, j, t: (0, 0, 0)),
+            pl.BlockSpec(wc.shape, lambda i, j, t: (0, 0, 0)),
         ],
         jax.ShapeDtypeStruct(parent_front.shape, F32),
         pl.BlockSpec((TILE, TILE), lambda i, j, t: (i, j)), "final",
-        scratch=[pltpu.VMEM((TILE, 2 * TILE), BF16)] * 2,
+        scratch=[pltpu.VMEM((n * TILE, 2 * TILE), BF16) for n in (rd, rd, cd, cd)],
     )
 
 

time: 375 us -> 268 us (0.71); the launches traced: 369 us -> 266 us
  waiting for transfers between devices: 145 us -> 20.9 us
  Pallas kernels: 107 us -> 214 us
  blocking collectives: 35.8 us -> 0 us
  matrix products: 16.3 us -> 0 us
  starting transfers between devices: 23.4 us -> 10.3 us
  between operations: 14.5 us -> 1.48 us
  local copies, waits for them, and re-layouts: 16.7 us -> 12.8 us
  other arithmetic: 10.7 us -> 6.85 us
    pallas_call x0 -> x5, Pallas kernels: none -> 123 us  [the longest x4 119 us: remote_call(): pl.pallas_call(kernel, out_shape=out_shape, in_specs=[pl.BlockSpec(memory...]
    all_gather x3 -> x0, waiting for transfers between devices: 86.7 us -> none  [the longest x1 69.2 us: body(): lax.all_gather(jnp.sum(diagonal, axis=0), every, axis=0, tiled=True)]
    all_to_all x3 -> x1, waiting for transfers between devices: 41.5 us -> 0.01 us  [body(): lax.all_to_all(coded, plane, split_axis=0, concat_axis=0, tiled=True)]
    all_to_all x1 -> x0, blocking collectives: 35.8 us -> none  [body(): lax.all_to_all(coded, ('child', 'rx'), split_axis=0, concat_axis=0, tiled...]
    all_to_all x1, waiting for transfers between devices: 0.01 us -> 20.9 us  [body(): lax.all_to_all(outgoing, 'col', split_axis=0, concat_axis=0, tiled=True)]
    pallas_call x1, Pallas kernels: 46 us -> 28.9 us  [factor_inverse(): pl.pallas_call(factor_kernel, out_shape=jax.ShapeDtypeStruct(d.shape, F32...]
    reduce_scatter x1 -> x0, waiting for transfers between devices: 16.7 us -> none  [body(): piece = lax.psum_scatter(strip_part, plane, scatter_dimension=0, tiled=True)]
    dot_general x2 -> x0, matrix products: 16.3 us -> none  [the longest x1 8.33 us: body(): lax.dot_general(inverse, strip, (((1,), (0,)), ((), ())), precision=lax.P...]
  transfers between devices with their start and end apart: 9 -> 3, of which waited for: 5 -> 1; matrix products, arithmetic and copies ran while one was open for 10% -> 5% of each run, Pallas kernels for 15% -> 63%
where the time goes in v1:
time: 268 us; the launch traced here: 266 us
  Pallas kernels  214 us (80%)
  waiting for transfers between devices  20.9 us (8%)
  local copies, waits for them, and re-layouts  12.8 us (5%)
  starting transfers between devices  10.3 us (4%)
  other arithmetic  6.85 us (3%)
    pallas_call x4, Pallas kernels, remote_call(): pl.pallas_call(kernel, out_shape=out_shape, in_specs=[pl.BlockSpec(memory...  119 us
    pallas_call x5, Pallas kernels, tile_call(): pl.pallas_call(kernel, grid_spec=pltpu.PrefetchScalarGridSpec(num_scalar_...  61.9 us
    pallas_call x1, Pallas kernels, factor_inverse(): pl.pallas_call(factor_kernel, out_shape=jax.ShapeDtypeStruct(d.shape, F32...  28.9 us
    all_to_all x1, waiting for transfers between devices, body(): lax.all_to_all(outgoing, 'col', split_axis=0, concat_axis=0, tiled=True)  20.9 us
    all_to_all x1, starting transfers between devices, body(): lax.all_to_all(coded, plane, split_axis=0, concat_axis=0, tiled=True)  5.51 us
  transfers between devices with their start and end apart: 3, of which 1 were waited for; matrix products, arithmetic and copies ran while one was open for 5% of the time, Pallas kernels for 63%

profile of v1, /device:TPU:25, one launch (start us, length us, event | category | flops | bytes accessed | tf_op | source)
XLA Modules:
  0.0 266.2 jit_solution(4187276860017049544)
XLA Ops:
  0.0 0.9 select_reduce_fusion.1
  1.5 0.6 dynamic_slice.57
  2.7 0.6 dynamic_slice.56
  4.4 11.1 %pick.1 = s16[4,4,272,256]{3,2,1,0:T(8,128)(2,1)} custom-call(s32[4]{0:T(128)} %get-tuple-element.41.idx, f32[1024,1024]{1,0:T(8,128)} %bitcast.126), custom_call_target="tpu_custom_call" | custom-call | tf_op jit(solution)/shard_map/pick/pallas_call | solution.py:30
  15.5 1.9 select_bitcast_fusion.x
  17.4 4.7 %all-to-all-start = ((s16[4,4,272,256]{3,2,1,0:T(8,128)(2,1)}), s16[4,4,272,256]{3,2,1,0:T(8,128)(2,1)S(1)}, u32[]{:S(2)}, u32[]{:S(2)}) async-start(s16[4,4,272,256]{3,2,1,0:T(8,128)(2,1)} %pick.1), calls=%async_computation | async-start | bytes 4456448 | tf_op jit(solution)/shard_map/all_to_all | solution.py:509
  22.5 0.6 gather_fusion.2
  23.1 0.6 gather_fusion.3
  23.8 0.6 gather_fusion.4
  24.4 0.6 gather_fusion.5
  25.0 0.6 gather_fusion.6
  25.7 18.3 %panels.1.partner.eb = bf16[4,256,1024]{2,1,0:T(8,128)(2,1)} custom-call(bf16[256,1024]{1,0:T(8,128)(2,1)} %select_bitcast_fusion.x), custom_call_target="tpu_custom_call" | custom-call | bytes 1048576 | tf_op jit(solution)/shard_map/panels/pallas_call | solution.py:188
  44.3 0.6 gather_fusion
  45.6 0.6 gather_fusion.7
  46.4 0.6 fusion.23
  47.0 1.3 compare_select_fusion.4
  48.6 0.6 multiply_bitcast_fusion.fac
  49.2 20.9 %all-to-all-done.raw = s16[4,4,272,256]{3,2,1,0:T(8,128)(2,1)S(1)} async-done(((s16[4,4,272,256]{3,2,1,0:T(8,128)(2,1)}), s16[4,4,272,256]{3,2,1,0:T(8,128)(2,1)S(1)}, u32[]{:S(2)}, u32[]{:S(2)}) %all-to-all-start) | async-done | bytes 2228256 | tf_op jit(solution)/shard_map/all_to_all | solution.py:509
  70.2 1.3 copy-done.2
  71.5 15.5 %update.1 = (f32[4,256,1024]{2,1,0:T(8,128)}, s16[4,2,272,512]{3,2,1,0:T(8,128)(2,1)}) custom-call(s32[4]{0:T(128)} %get-tuple-element.43.rows, s32[4,4]{1,0:T(4,128)} %multiply_bitcast_fusion.fac, s16[4,4,272,256]{3,2,1,0:T(8,128)(2,1)} %copy-done.2, bf16[1024,1024]{1,0:T(8,128)(2,1)} %bitcast.128, bf16[4,256,1024]{2,1,0:T(8,128)(2,1)} %panels.1.partner.eb), custom_call_target="tpu_custom_call" | custom-call | tf_op jit(solution)/shard_map/update/pallas_call | solution.py:30
  87.0 5.5 %all-to-all-start.1 = ((s16[8,272,512]{2,1,0:T(8,128)(2,1)}), s16[8,272,512]{2,1,0:T(8,128)(2,1)S(1)}, u32[]{:S(2)}, u32[]{:S(2)}) async-start(s16[8,272,512]{2,1,0:T(8,128)(2,1)} %bitcast.131), calls=%async_computation.1 | async-start | bytes 4456448 | tf_op jit(solution)/shard_map/all_to_all | solution.py:556
  93.2 0.6 stack.91.t
  93.8 5.4 %diag.1 = f32[512,512]{1,0:T(8,128)} custom-call(s32[8,4]{1,0:T(8,128)} %stack.91.t, f32[1024,1024]{1,0:T(8,128)} %bitcast.127, f32[768,1536]{1,0:T(8,128)} %front.5, bf16[1024,1024]{1,0:T(8,128)(2,1)} %bitcast.129, bf16[4,256,1024]{2,1,0:T(8,128)(2,1)} %panels.1.partner.eb), custom_call_target="tpu_custom_call" | custom-call | tf_op jit(solution)/shard_map/diag/pallas_call | solution.py:30
  99.2 43.0 %total.1 = f32[2,4,4,16,512]{4,3,2,1,0:T(8,128)} custom-call(f32[2,4,4,16,512]{4,3,2,1,0:T(8,128)} %bitcast.130), custom_call_target="tpu_custom_call" | custom-call | bytes 1048576 | tf_op jit(solution)/shard_map/total/pallas_call | solution.py:188
  143.7 0.6 stack.90.t
  144.3 1.2 stack.89.t
  145.7 28.9 %factor.1.inverse = f32[512,512]{1,0:T(8,128)} custom-call(f32[512,512]{1,0:T(8,128)} %bitcast.132), custom_call_target="tpu_custom_call" | custom-call | flops 40000000000 | bytes 2097152 | tf_op jit(solution)/shard_map/factor/pallas_call | solution.py:446
  174.5 10.5 %strip.1.x = s16[8,208,512]{2,1,0:T(8,128)(2,1)} custom-call(s32[5,12]{1,0:T(8,128)} %stack.90.t, f32[4,256,1024]{2,1,0:T(8,128)} %get-tuple-element.14.upd, f32[768,1536]{1,0:T(8,128)} %front.5), custom_call_target="tpu_custom_call" | custom-call | tf_op jit(solution)/shard_map/strip/pallas_call | solution.py:30
  185.1 23.2 %strips.1.parts = s16[8,208,512]{2,1,0:T(8,128)(2,1)} custom-call(s16[8,208,512]{2,1,0:T(8,128)(2,1)} %strip.1.x), custom_call_target="tpu_custom_call" | custom-call | bytes 1048576 | tf_op jit(solution)/shard_map/strips/pallas_call | solution.py:188
  208.3 4.2 %solve.1.x = s16[208,512]{1,0:T(8,128)(2,1)} custom-call(s16[8,208,512]{2,1,0:T(8,128)(2,1)} %strips.1.parts, f32[512,512]{1,0:T(8,128)} %factor.1.inverse), custom_call_target="tpu_custom_call" | custom-call | tf_op jit(solution)/shard_map/solve/pallas_call | solution.py:581
  212.5 34.3 %spread.1 = (s16[8,208,512]{2,1,0:T(8,128)(2,1)}, s16[4,208,512]{2,1,0:T(8,128)(2,1)}) custom-call(s16[208,512]{1,0:T(8,128)(2,1)} %solve.1.x), custom_call_target="tpu_custom_call" | custom-call | bytes 1048576 | tf_op jit(solution)/shard_map/spread/pallas_call | solution.py:188
  246.8 19.4 %final.1 = f32[768,1536]{1,0:T(8,128)} custom-call(s32[13,18]{1,0:T(8,128)} %stack.89.t, f32[768,1536]{1,0:T(8,128)} %front.5, s16[8,272,512]{2,1,0:T(8,128)(2,1)} %copy-done.1, s16[8,272,512]{2,1,0:T(8,128)(2,1)} %collective-permute-done.b0.b1, s16[8,272,512]{2,1,0:T(8,128)(2,1)} %copy-done.1, s16[8,272,512]{2,1,0:T(8,128)(2,1)} %collective-permute-done.b0.b1, ...), custom_call_target="tpu_custom_call" | custom-call | tf_op jit(solution)/shard_map/final/pallas_call | solution.py:30
  (87 shorter events, 5.1 us)
Async XLA Ops:
  0.0 44.3 %copy-start = (s32[2,16,16]{2,1,0:T(8,128)S(1)}, s32[2,16,16]{2,1,0:T(8,128)}, u32[]{:S(2)}) copy-start(s32[2,16,16]{2,1,0:T(8,128)} %param.10) | copy-start | bytes 6148
  17.4 4.9 %copy-start.3 = (s32[24]{0:T(128)S(1)}, s32[24]{0:T(128)}, u32[]{:S(2)}) copy-start(s32[24]{0:T(128)} %param.12) | copy-start | bytes 292
  17.4 5.0 %copy-start.5 = (s32[4]{0:T(128)S(1)}, s32[4]{0:T(128)}, u32[]{:S(2)}) copy-start(s32[4]{0:T(128)} %constant.302) | copy-start | bytes 52
  17.4 5.0 %copy-start.4 = (s32[4]{0:T(128)S(1)}, s32[4]{0:T(128)}, u32[]{:S(2)}) copy-start(s32[4]{0:T(128)} %constant.303) | copy-start | bytes 52
  17.4 52.7 %all-to-all-start = ((s16[4,4,272,256]{3,2,1,0:T(8,128)(2,1)}), s16[4,4,272,256]{3,2,1,0:T(8,128)(2,1)S(1)}, u32[]{:S(2)}, u32[]{:S(2)}) async-start(s16[4,4,272,256]{3,2,1,0:T(8,128)(2,1)} %pick.1), calls=%async_computation | async-start | bytes 4456448 | tf_op jit(solution)/shard_map/all_to_all | solution.py:509
  70.2 1.3 copy-start.2
  87.0 58.5 %all-to-all-start.1 = ((s16[8,272,512]{2,1,0:T(8,128)(2,1)}), s16[8,272,512]{2,1,0:T(8,128)(2,1)S(1)}, u32[]{:S(2)}, u32[]{:S(2)}) async-start(s16[8,272,512]{2,1,0:T(8,128)(2,1)} %bitcast.131), calls=%async_computation.1 | async-start | bytes 4456448 | tf_op jit(solution)/shard_map/all_to_all | solution.py:556
  145.6 29.0 %copy-start.1 = (s16[8,272,512]{2,1,0:T(8,128)(2,1)}, s16[8,272,512]{2,1,0:T(8,128)(2,1)S(1)}, u32[]{:S(2)}) copy-start(s16[8,272,512]{2,1,0:T(8,128)(2,1)S(1)} %all-to-all-done.1.a0.a1) | copy-start | bytes 6684676
  145.6 101.3 %collective-permute-start = (s16[8,272,512]{2,1,0:T(8,128)(2,1)S(1)}, s16[8,272,512]{2,1,0:T(8,128)(2,1)}, u32[]{:S(2)}, u32[]{:S(2)}) collective-permute-start(s16[8,272,512]{2,1,0:T(8,128)(2,1)S(1)} %all-to-all-done.1.a0.a1), channel_id=1, source_target_pairs={{0,4},{4,0},{1,5},{5,1},{2,6},{6,2},{3,7},{7,3},{8,12},{12,8},{9,1... | collective-permute-start | bytes 6684680 | tf_op jit(solution)/shard_map/ppermute | solution.py:557

commit v2 on v1

--- a/solution.py
+++ b/solution.py
@@ -1,4 +1,5 @@
 import functools
+import math
 
 import jax
 import jax.numpy as jnp
@@ -64,10 +65,93 @@
     return q * (meta[1:2, :] * (1.0 / (FULL * FULL)) * p) * r
 
 
-def pick_kernel(idx, src, out):
-    q, meta = encode(src[...])
-    out[0, 0, :TILE, :] = q
-    out[0, 0, TILE:, :] = meta
+def find(maps, place, child, block, group, td, width):
+    at = jnp.int32(0)
+    ok = jnp.int32(0)
+    for t in range(td):
+        hit = place[maps[child, block * td + t]] // width == group
+        at = jnp.where(hit, t, at)
+        ok = jnp.where(hit, 1, ok)
+    return at, ok
+
+
+def pick_kernel(td, cd, pos, maps, place, src, panel, out, part):
+    n = out.shape[1]
+    for r in range(n):
+        q, meta = encode(src[r * TILE : (r + 1) * TILE, :])
+        out[0, r, :TILE, :] = q
+        out[0, r, TILE:, :] = meta
+
+    @pl.when(pl.program_id(0) == 0)
+    def _():
+        ok = find(maps, place, pos[0], pos[1], pos[2], td, cd)[1]
+        part[...] = jnp.where(ok != 0, panel[...], jnp.zeros_like(panel))
+
+
+def plan_kernel(dims, pos, maps, place, pat, rowt, fac, diagt, stript, fint, inv):
+    td, cd, rd, chips, blocks, cores, rown = dims
+    ci, row, col, core = pos[0], pos[1], pos[2], pos[3]
+    group = ci * rown + row
+    wide = blocks // cores
+    slots_n, tiles_n = place.shape[0], maps.shape[1]
+
+    @pl.loop(0, slots_n)
+    def _(k):
+        inv[0, k] = -1
+        inv[1, k] = -1
+
+    @pl.loop(0, tiles_n)
+    def _(k):
+        inv[0, place[maps[0, k]]] = k
+        inv[1, place[maps[1, k]]] = k
+
+    cols = [find(maps, place, ci, b, col, td, cd) for b in range(blocks)]
+    for x in range(chips):
+        at, ok = find(maps, place, ci, row, x, td, cd)
+        rowt[x] = at
+        for b, (tile, good) in enumerate(cols):
+            fac[x, b] = pat[ci, row * td + at, b * td + tile] * ok * good
+    e = (place[0], place[1])
+    ie = (inv[ci, e[0]], inv[ci, e[1]])
+    le = [jnp.maximum(i, 0) for i in ie]
+    own = [((ie[a] >= 0) & (le[a] // td == row)).astype(jnp.int32) for a in range(2)]
+    for a in range(2):
+        rowt[chips + a] = jnp.where(own[a] != 0, e[a] // cd, -1)
+        for b in range(2):
+            k = a * 2 + b
+            live = own[a] * (ie[b] >= 0).astype(jnp.int32) * pat[ci, le[a], le[b]]
+            diagt[0, k] = le[a] % td
+            diagt[1, k] = le[b] % td
+            diagt[2, k] = e[a] % rd
+            diagt[3, k] = e[b] % cd
+            diagt[4, k] = live * (le[b] // td == col).astype(jnp.int32)
+            diagt[5, k] = ((e[a] // rd == group) & (e[b] // cd == col)).astype(jnp.int32)
+            diagt[6, k] = live * (e[b] // cd == col).astype(jnp.int32)
+            diagt[7, k] = le[b] // td
+        stript[0, a] = e[a] % rd
+
+        for q in range(cd):
+            slot = col * cd + q
+            iq = inv[ci, slot]
+            free = ((slot != e[0]) & (slot != e[1])).astype(jnp.int32)
+            stript[1 + a, q] = jnp.maximum(iq, 0) // td
+            stript[3 + a, q] = own[a] * free * (iq >= 0).astype(jnp.int32)
+            stript[5 + a, q] = free * (e[a] // rd == group).astype(jnp.int32)
+    for k in range(2, cd):
+        stript[0, k] = 0
+
+    @pl.loop(0, rd * cd)
+    def _(k):
+        slot = col * cd + k % cd
+        for c in range(2):
+            r, t = inv[c, group * rd + k // cd], inv[c, slot]
+            ok = ((r >= 0) & (t >= 0)).astype(jnp.int32)
+            b = jnp.maximum(t, 0) // td
+            same = (b // wide == core).astype(jnp.int32)
+            fint[3 * c, k] = c * rown + jnp.maximum(r, 0) // td
+            fint[3 * c + 1, k] = b % wide
+            fint[3 * c + 2, k] = ok * (2 - same)
+        fint[6, k] = jnp.where(slot == e[0], 1, jnp.where(slot == e[1], 2, 0))
 
 
 def diag_kernel(t, blk, front, ea, eb, out):
@@ -76,50 +160,88 @@
     out[...] = x - jnp.where(t[6, k] != 0, dot(ea[...], eb[0], NT), 0.0)
 
 
-def update_kernel(rows, fac, raw, panel, partner, out, coded):
-    f = fac[pl.program_id(0), pl.program_id(1)]
-    u = decode(raw[0, 0]) - dot(panel[...], partner[0], NT)
-    u = jnp.where(f != 0, u, 0.0)
-    out[0] = u
-    q, meta = encode(u)
-    coded[0, 0, :TILE, :] = q
-    coded[0, 0, TILE:, :] = meta
-
-
-def strip_kernel(t, upd, front, out, g):
-    a, q = pl.program_id(0), pl.program_id(1)
-    cd = pl.num_programs(1)
-    k = a * cd + q
-    x = jnp.where(t[2, k] != 0, upd[0], 0.0) + jnp.where(t[4, k] != 0, front[...], 0.0)
-    rows = pl.ds(pl.multiple_of(q * TILE, TILE), TILE)
-    g[rows, pl.ds(pl.multiple_of(a * TILE, TILE), TILE)] = x.T
-
-    @pl.when(jnp.logical_and(a == 1, q == cd - 1))
+def update_kernel(rowt, fac, raw, panel, partner, strip, coded):
+    p = pl.program_id(0)
+    chips = pl.num_programs(0)
+    blocks = partner.shape[0]
+    wide = coded.shape[3] // TILE
+
+    @pl.when(p == 0)
     def _():
-        n = out.shape[1] - META
-        for p in range(out.shape[0]):
-            code, meta = encode(g[p * n : (p + 1) * n, :])
-            out[p, :n, :] = code
-            out[p, n:, :] = meta
-
-
-def solve_kernel(parts, inverse, out):
+        strip[...] = jnp.zeros_like(strip)
+
+    for b in range(blocks):
+        u = decode(raw[b, 0]) - dot(panel[...], partner[b], NT)
+        u = jnp.where(fac[p, b] != 0, u, 0.0)
+        at = slice(b % wide * TILE, (b % wide + 1) * TILE)
+        q, meta = encode(u)
+        coded[0, b // wide, :TILE, at] = q
+        coded[0, b // wide, TILE:, at] = meta
+        for a in range(2):
+
+            @pl.when(rowt[chips + a] == p)
+            def _(a=a, u=u, b=b):
+                strip[a, :, b * TILE : (b + 1) * TILE] = u
+
+
+def strip_kernel(t, upd, f0, f1, out, g):
+    cd = t.shape[1]
+    some = sum(t[n, q] for n in range(3, 7) for q in range(cd))
+
+    @pl.when(some == 0)
+    def _():
+        out[...] = jnp.zeros_like(out)
+
+    @pl.when(some != 0)
+    def _():
+        g[...] = jnp.zeros_like(g)
+        for q in range(cd):
+            for a, f in enumerate((f0, f1)):
+
+                @pl.when(t[3 + a, q] + t[5 + a, q] != 0)
+                def _(q=q, a=a, f=f):
+                    at = pl.ds(pl.multiple_of(t[1 + a, q] * TILE, TILE), TILE)
+                    x = jnp.where(t[3 + a, q] != 0, upd[a, :, at], 0.0)
+                    x = x + jnp.where(t[5 + a, q] != 0, f[:, q * TILE : (q + 1) * TILE], 0.0)
+                    g[q * TILE : (q + 1) * TILE, a * TILE : (a + 1) * TILE] = x.T
+
+        n = out.shape[2] - META
+        for p in range(out.shape[1]):
+            for k in range(out.shape[0]):
+                m = p * out.shape[0] + k
+                code, meta = encode(g[m * n : (m + 1) * n, :])
+                out[k, p, :n, :] = code
+                out[k, p, n:, :] = meta
+
+
+def solve_kernel(pos, place, parts, diagonal, inverse, out):
+    n = out.shape[0] - META
     g = decode(parts[0])
     for p in range(1, parts.shape[0]):
         g = g + decode(parts[p])
+    unit = math.gcd(n, TILE)
+    rows = []
+    for u in range(n // unit):
+        first = pos[4] * n + u * unit
+        slot, off = first // TILE, first % TILE
+        x = g[u * unit : (u + 1) * unit, :]
+        for a in range(2):
+            d = diagonal[pl.ds(pl.multiple_of(a * TILE + off, unit), unit), :]
+            x = jnp.where(pos[5] + slot == place[a], d, x)
+        rows.append(x)
+    g = jnp.concatenate(rows, axis=0)
     w = lax.dot_general(g, inverse[...], NT, precision=lax.Precision.HIGHEST, preferred_element_type=F32)
-    n = out.shape[0] - META
     code, meta = encode(w)
     out[:n, :] = code
     out[n:, :] = meta
 
 
-def final_kernel(t, front, a0, b0, a1, b1, wr, wc, out, rh, rl, ch, cl):
+def final_kernel(t, front, first, second, wr, wc, out, rh, rl, ch, cl):
     i, j = pl.program_id(0), pl.program_id(1)
-    k = i * pl.num_programs(1) + j
-    panel = t[12, k]
-
-    @pl.when(k == 0)
+    per = out.shape[1] // TILE
+    base = (i * pl.num_programs(1) + j) * per
+
+    @pl.when(base == 0)
     def _():
         for src, hi, lo in ((wr, rh, rl), (wc, ch, cl)):
             n = src.shape[1] - META
@@ -128,25 +250,27 @@
                 hi[at, :], lo[at, :] = split(decode(src[p]))
 
     ri = pl.ds(pl.multiple_of(i * TILE, TILE), TILE)
-
-    @pl.when(panel == 0)
-    def _():
-        cj = pl.ds(pl.multiple_of(j * TILE, TILE), TILE)
-        big = dot(rh[ri, :], ch[cj, :], NT)
-        out[...] = front[...] - (big + (dot(rh[ri, :], cl[cj, :], NT) + dot(rl[ri, :], ch[cj, :], NT)))
-        for m, src in enumerate((a0, b0, a1, b1)):
-
-            @pl.when(t[8 + m, k] != 0)
-            def _(src=src):
-                out[...] = out[...] + decode(src[0])
-
-    @pl.when(panel == 1)
-    def _():
-        out[...] = rh[ri, :TILE].astype(F32) + rl[ri, :TILE].astype(F32)
-
-    @pl.when(panel == 2)
-    def _():
-        out[...] = rh[ri, TILE:].astype(F32) + rl[ri, TILE:].astype(F32)
+    cj = pl.ds(pl.multiple_of(j * TILE * per, TILE), TILE * per)
+    wh, wl = rh[ri, :], rl[ri, :]
+    big = dot(wh, ch[cj, :], NT)
+    out[...] = front[...] - (big + (dot(wh, cl[cj, :], NT) + dot(wl, ch[cj, :], NT)))
+    for m in range(per):
+        k = base + m
+        at = slice(m * TILE, (m + 1) * TILE)
+        for c in range(2):
+            for n, src in enumerate((first, second)):
+
+                @pl.when(t[3 * c + 2, k] == n + 1)
+                def _(src=src, c=c, k=k, at=at):
+                    lanes = pl.ds(pl.multiple_of(t[3 * c + 1, k] * TILE, TILE), TILE)
+                    out[:, at] = out[:, at] + decode(src[t[3 * c, k], :, lanes])
+
+        for n in range(2):
+
+            @pl.when(t[6, k] == n + 1)
+            def _(n=n, at=at):
+                half = slice(n * TILE, (n + 1) * TILE)
+                out[:, at] = rh[ri, half].astype(F32) + rl[ri, half].astype(F32)
 
 
 MESH = pl.DeviceIdType.MESH
@@ -280,26 +404,40 @@
     return out.reshape(n, n)
 
 
-def scatter_kernel(x, out, loc, ss, rs):
+def scatter_kernel(x, out, half, mine, ss, rs, cs, cr):
     s = Spot()
-    n = x.shape[0]
-    me = s.chip * s.cores + s.core
-    peers = [s.turn(me, d, n) for d in range(1, n)]
-    ids = [s.id(t // s.cores, lax.rem(t, s.cores)) for t in peers]
-    greet(ids)
-    keep = pltpu.make_async_copy(x.at[me], out.at[me], loc)
-    keep.start()
-    cps = [push(x.at[t], out.at[me], ss.at[d], rs.at[d], i) for d, (t, i) in enumerate(zip(peers, ids))]
-    keep.wait()
+    nc = s.chips
+    n = x.shape[2] - META
+    order = [s.turn(s.chip, d, nc) for d in range(1, nc + 1)]
+    greet([s.other] + [s.id(t) for t in order[:-1]])
+    pairs = [push(x.at[1 - s.core, t], half.at[t], ss.at[d], rs.at[t], s.other) for d, t in enumerate(order)]
+    cps = []
+    for d, t in enumerate(order):
+        pltpu.make_async_remote_copy(
+            src_ref=half.at[t], dst_ref=half.at[t], send_sem=ss.at[d], recv_sem=rs.at[t],
+            device_id=s.other, device_id_type=MESH,
+        ).wait_recv()
+        q, meta = encode(decode(x[s.core, t]) + decode(half[t]))
+        if d < nc - 1:
+            mine[d, :n, :] = q
+            mine[d, n:, :] = meta
+            cps.append(push(mine.at[d], out.at[d + 1], cs.at[d], cr.at[d], s.id(t)))
+        else:
+            out[0, :n, :] = q
+            out[0, n:, :] = meta
+    for cp in pairs:
+        cp.wait_send()
     for cp in cps:
         cp.wait()
 
 
 def scatter(x):
-    n = x.shape[0]
+    nc = x.shape[1]
     dma = pltpu.SemaphoreType.DMA
+    shape = x.shape[1:]
     return remote_call(
-        scatter_kernel, (x,), jax.ShapeDtypeStruct(x.shape, x.dtype), ANY, [dma, dma((n,)), dma((n,))], 2, "strips"
+        scatter_kernel, (x,), jax.ShapeDtypeStruct(shape, x.dtype), IN_VMEM,
+        [pltpu.VMEM(shape, x.dtype)] * 2 + [dma((nc,))] * 4, 2, "strips"
     )
 
 
@@ -310,12 +448,10 @@
     slot = lax.rem(me, half)
     n = nc * s.cores
     chips = [s.turn(s.chip, d, nc) for d in range(1, nc)]
-    cols = [s.turn(s.col, d, nz) for d in range(1, nz)]
     plane = [s.turn(me, d, n) for d in range(1, n)]
-    greet([s.id(t // s.cores, lax.rem(t, s.cores)) for t in plane] + [{"col": t} for t in cols])
+    greet([s.id(t // s.cores, lax.rem(t, s.cores)) for t in plane] + [{"col": s.turn(s.col, d, nz)} for d in range(1, nz)])
     keep = pltpu.make_async_copy(x, wc.at[me], loc)
     keep.start()
-    zc = [push(x, zbuf.at[s.col], zs.at[d], zr.at[d], {"col": t}) for d, t in enumerate(cols, 1)]
     pc = [push(x, wc.at[me], ps.at[d], pr.at[d], s.id(t)) for d, t in enumerate(chips, 1)]
     fc = [push(x, wc.at[me], fs.at[0], fr.at[0], s.other)]
 
@@ -344,18 +480,64 @@
                 device_id=s.id(z, s.ci), device_id_type=MESH,
             ).wait_send()
 
+    def hop(src, z, way, d):
+        to = s.col + way
+
+        @pl.when(jnp.logical_and(to >= 0, to < nz))
+        def _():
+            push(src, zbuf.at[z], zs.at[d], zr.at[z], {"col": to})
+
+    def hopped(src, z, way, d):
+        to = s.col + way
+
+        @pl.when(jnp.logical_and(to >= 0, to < nz))
+        def _():
+            pltpu.make_async_remote_copy(
+                src_ref=src, dst_ref=zbuf.at[z], send_sem=zs.at[d], recv_sem=zr.at[z],
+                device_id={"col": to}, device_id_type=MESH,
+            ).wait_send()
+
+    hop(x, s.col, 1, 0)
+    hop(x, s.col, -1, 1)
     hand(x, s.col, 0)
-    back = [s.turn(s.col, -d, nz) for d in range(nz)]
+
+    def moved(d, way):
+        z = s.col - way * d
+        n = 2 * d + (way < 0)
+
+        @pl.when(jnp.logical_and(z >= 0, z < nz))
+        def _():
+            src = zbuf.at[z]
+            pltpu.make_async_remote_copy(
+                src_ref=src, dst_ref=src, send_sem=zs.at[n], recv_sem=zr.at[z],
+                device_id=s.other, device_id_type=MESH,
+            ).wait_recv()
+            hop(src, z, way, n)
+            hand(src, z, n)
+
+    def done(d, way):
+        z = s.col - way * d
+        n = 2 * d + (way < 0)
+
+        @pl.when(jnp.logical_and(z >= 0, z < nz))
+        def _():
+            hopped(zbuf.at[z], z, way, n)
+            handed(zbuf.at[z], z, n)
+
     for d in range(1, max(nz, nc)):
         if d < nz:
-            zc[d - 1].wait_recv()
-            hand(zbuf.at[back[d]], back[d], d)
+            moved(d, 1)
+            moved(d, -1)
         if d < nc:
             pc[d - 1].wait_recv()
             at = s.turn(s.chip, -d, nc) * s.cores + s.core
             fc.append(push(wc.at[at], wc.at[at], fs.at[d], fr.at[d], s.other))
-    for d in range(nz):
-        handed(x if d == 0 else zbuf.at[back[d]], back[d], d)
+    hopped(x, s.col, 1, 0)
+    hopped(x, s.col, -1, 1)
+    handed(x, s.col, 0)
+    for d in range(1, nz):
+        done(d, 1)
+        done(d, -1)
     for j in range(half):
 
         @pl.when(jnp.logical_or(s.ci != s.core, slot != j))
@@ -366,7 +548,7 @@
             ).wait_recv()
 
     keep.wait()
-    for cp in zc + pc:
+    for cp in pc:
         cp.wait_send()
     for cp in fc:
         cp.wait()
@@ -375,7 +557,7 @@
 def spread(x):
     nc, nz = lax.axis_size(("child", "rx")), lax.axis_size("col")
     dma = pltpu.SemaphoreType.DMA
-    sems = [dma] + [dma((nz,))] * 2 + [dma((nc,))] * 4 + [dma((nz,)), dma((nc,)), dma]
+    sems = [dma, dma((2 * nz,)), dma((nz,))] + [dma((nc,))] * 4 + [dma((2 * nz,)), dma((nc,)), dma]
     shapes = [jax.ShapeDtypeStruct((n,) + x.shape, x.dtype) for n in (2 * nc, nc)]
     return remote_call(
         spread_kernel, (x,), shapes, [ANY, ANY], [pltpu.VMEM((nz,) + x.shape, x.dtype)] + sems, 3, "spread"
@@ -475,51 +657,44 @@
     slots_n = parent_place.shape[0]
     i32 = jnp.int32
 
-    slots = jnp.sum(
-        jnp.where(child_maps[:, :, None] == jnp.arange(slots_n, dtype=i32), parent_place, 0), axis=2
-    )
-    tiles = jnp.arange(child_maps.shape[1], dtype=i32)
-    hit = slots[:, None, :] == jnp.arange(slots_n, dtype=i32)[None, :, None]
-    inv = jnp.sum(jnp.where(hit, tiles + 1, 0), axis=2) - 1
-    mine = lax.dynamic_index_in_dim(slots, ci, 0, keepdims=False).reshape(blocks, td)
-    inv_own = lax.dynamic_index_in_dim(inv, ci, 0, keepdims=False)
-    pat = lax.dynamic_index_in_dim(child_patterns, ci, 0, keepdims=False)
-    m = (mine // cd)[:, None, :] == jnp.arange(chips, dtype=i32)[None, :, None]
-    which = jnp.sum(jnp.where(m, jnp.arange(td, dtype=i32), 0), axis=2)
-    there = jnp.any(m, axis=2).astype(i32)
-    row_tile = lax.dynamic_index_in_dim(which, row, 0, keepdims=False)
-    row_ok = lax.dynamic_index_in_dim(there, row, 0, keepdims=False)
-    out_tile = lax.dynamic_index_in_dim(which, col, 0, keepdims=False)
-    in_tile = lax.dynamic_index_in_dim(which, col, 1, keepdims=False)
-    in_ok = lax.dynamic_index_in_dim(there, col, 1, keepdims=False)
-    e = parent_place[:2]
-    ie = inv_own[e]
-
-    outgoing = tile_call(
-        pick_kernel, (blocks, td), (out_tile,), (block,),
-        [pl.BlockSpec((TILE, TILE), lambda z, r, i: (r, i[z]))],
-        jax.ShapeDtypeStruct((blocks, td, CODED, TILE), jnp.int16),
-        pl.BlockSpec((1, 1, CODED, TILE), lambda z, r, i: (z, r, 0, 0)), "pick",
-    )
-    part = lax.dynamic_slice(own, (row_tile[col] * TILE, 0), (TILE, depth))
-    part = jnp.where(row_ok[col] != 0, part, jnp.zeros_like(part))
-
-    e_here = jnp.logical_and(ie >= 0, ie // td == row)
-    part, outgoing = lax.optimization_barrier((part, outgoing))
+    share = cd * TILE // (chips * cores)
+    wide = blocks // cores
+    me = chip * cores + core
+    pos = jnp.stack([ci, row, col, core, me, col * cd]).astype(i32)
+
+    def tile_at(block, group, pos, maps, place):
+        return find(maps, place, pos[0], block, group, td, cd)[0]
+
+    outgoing, part = tile_call(
+        functools.partial(pick_kernel, td, cd), (blocks,), (pos, child_maps, parent_place), (block, own),
+        [
+            pl.BlockSpec((width, TILE), lambda z, pos, maps, place: (0, tile_at(pos[2], z, pos, maps, place))),
+            pl.BlockSpec((TILE, depth), lambda z, pos, maps, place: (tile_at(pos[1], pos[2], pos, maps, place), 0)),
+        ],
+        [
+            jax.ShapeDtypeStruct((blocks, td, CODED, TILE), jnp.int16),
+            jax.ShapeDtypeStruct((TILE, depth), own.dtype),
+        ],
+        [
+            pl.BlockSpec((1, td, CODED, TILE), lambda z, *_: (z, 0, 0, 0)),
+            pl.BlockSpec((TILE, depth), lambda z, *_: (0, 0)),
+        ], "pick",
+    )
     raw = lax.all_to_all(outgoing, "col", split_axis=0, concat_axis=0, tiled=True)
+
+    smem = pl.BlockSpec(memory_space=pltpu.SMEM)
+    dims = (td, cd, rd, chips, blocks, cores, rown)
+    sizes = [(chips + 2,), (chips, blocks), (8, 4), (7, cd), (7, rd * cd)]
+    rowt, fac, diagt, stript, fint = pl.pallas_call(
+        functools.partial(plan_kernel, dims),
+        in_specs=[smem] * 4, out_specs=[smem] * 5, name="plan",
+        out_shape=[jax.ShapeDtypeStruct(z, i32) for z in sizes],
+        scratch_shapes=[pltpu.SMEM((2, slots_n), i32)],
+    )(pos, child_maps, parent_place, child_patterns)
+
     partner = panel_gather(part)
-    pair_a = jnp.array([0, 0, 1, 1], i32)
-    pair_b = jnp.array([0, 1, 0, 1], i32)
-    ia, ib, ea, eb = ie[pair_a], ie[pair_b], e[pair_a], e[pair_b]
-    live = (ia >= 0) & (ib >= 0) & (pat[jnp.maximum(ia, 0), jnp.maximum(ib, 0)] != 0)
-    table = jnp.stack([
-        jnp.maximum(ia, 0) % td, jnp.maximum(ib, 0) % td, ea % rd, eb % cd,
-        live & (ia // td == row) & (ib // td == col),
-        (ea // rd == group) & (eb // cd == col),
-        live & (ia // td == row) & (eb // cd == col), jnp.maximum(ib, 0) // td,
-    ]).astype(i32)
     diag_part = tile_call(
-        diag_kernel, (2, 2), (table,), (block, parent_front, own, partner),
+        diag_kernel, (2, 2), (diagt,), (block, parent_front, own, partner),
         [
             pl.BlockSpec((TILE, TILE), lambda a, b, t: (t[0, a * 2 + b], t[1, a * 2 + b])),
             pl.BlockSpec((TILE, TILE), lambda a, b, t: (t[2, a * 2 + b], t[3, a * 2 + b])),
@@ -531,90 +706,62 @@
     )
     plane = ("child", "rx", "core")
     diagonal = sum_all(diag_part)
-    inverse = factor_inverse(diagonal)
-
-    wide = blocks // cores
-    col_ids = jnp.arange(blocks, dtype=i32) * td + in_tile
-    factors = pat[row * td + row_tile][:, col_ids] * row_ok[:, None] * in_ok[None, :]
-    update, coded = tile_call(
-        update_kernel, (chips, blocks), (row_tile, factors), (raw, own, partner),
-        [
-            pl.BlockSpec((1, 1, CODED, TILE), lambda p, b, r, f: (b, r[p], 0, 0)),
-            pl.BlockSpec((TILE, depth), lambda p, b, r, f: (r[p], 0)),
-            pl.BlockSpec((1, TILE, depth), lambda p, b, r, f: (b, 0, 0)),
+    diagonal, raw = lax.optimization_barrier((diagonal, raw))
+
+    strip_rows, coded = tile_call(
+        update_kernel, (chips,), (rowt, fac), (raw, own, partner),
+        [
+            pl.BlockSpec((blocks, 1, CODED, TILE), lambda p, r, f: (0, r[p], 0, 0)),
+            pl.BlockSpec((TILE, depth), lambda p, r, f: (r[p], 0)),
+            pl.BlockSpec((blocks, TILE, depth), lambda p, r, f: (0, 0, 0)),
         ],
         [
-            jax.ShapeDtypeStruct((chips, TILE, blocks * TILE), F32),
+            jax.ShapeDtypeStruct((2, TILE, blocks * TILE), F32),
             jax.ShapeDtypeStruct((chips, cores, CODED, wide * TILE), jnp.int16),
         ],
         [
-            pl.BlockSpec((1, TILE, TILE), lambda p, b, r, f: (p, 0, b)),
-            pl.BlockSpec((1, 1, CODED, TILE), lambda p, b, r, f: (p, b // wide, 0, b % wide)),
+            pl.BlockSpec((2, TILE, blocks * TILE), lambda p, r, f: (0, 0, 0)),
+            pl.BlockSpec((1, cores, CODED, wide * TILE), lambda p, r, f: (p, 0, 0, 0)),
         ], "update",
     )
     coded = coded.reshape((chips * cores,) + coded.shape[2:])
     first = lax.all_to_all(coded, plane, split_axis=0, concat_axis=0, tiled=True)
+    diagonal, coded = lax.optimization_barrier((diagonal, coded))
+    inverse = factor_inverse(diagonal)
+    first, inverse = lax.optimization_barrier((first, inverse))
     second = lax.ppermute(first, "core", [(k, (k + 1) % 2) for k in range(2)])
 
-    my_cols = lax.dynamic_slice_in_dim(inv, col * cd, cd, 1)
-    my_rows = lax.dynamic_slice_in_dim(inv, group * rd, rd, 1)
-    cols_own = lax.dynamic_index_in_dim(my_cols, ci, 0, keepdims=False)
-    grid_q = jnp.broadcast_to(jnp.arange(cd, dtype=i32), (2, cd))
-    e2 = jnp.broadcast_to(e[:, None], (2, cd))
-    cols2 = jnp.broadcast_to(cols_own[None, :], (2, cd))
-    table = jnp.stack([
-        e2 // cd, jnp.maximum(cols2, 0) // td,
-        (e_here[:, None] & (cols2 >= 0)),
-        e2 % rd, (e2 // rd == group),
-    ]).astype(i32).reshape(5, 2 * cd)
-    share = cd * TILE // (chips * cores)
+    pieces = (cores, chips, share + META, 2 * TILE)
     strip_part = tile_call(
-        strip_kernel, (2, cd), (table,), (update, parent_front),
-        [
-            pl.BlockSpec((1, TILE, TILE), lambda a, q, t: (t[0, a * cd + q], 0, t[1, a * cd + q])),
-            pl.BlockSpec((TILE, TILE), lambda a, q, t: (t[3, a * cd + q], q)),
+        strip_kernel, (1,), (stript,), (strip_rows, parent_front, parent_front),
+        [
+            pl.BlockSpec(strip_rows.shape, lambda k, t: (0, 0, 0)),
+            pl.BlockSpec((TILE, cd * TILE), lambda k, t: (t[0, 0], 0)),
+            pl.BlockSpec((TILE, cd * TILE), lambda k, t: (t[0, 1], 0)),
         ],
-        jax.ShapeDtypeStruct((chips * cores, share + META, 2 * TILE), jnp.int16),
-        pl.BlockSpec((chips * cores, share + META, 2 * TILE), lambda a, q, t: (0, 0, 0)), "strip",
+        jax.ShapeDtypeStruct(pieces, jnp.int16),
+        pl.BlockSpec(pieces, lambda k, t: (0, 0, 0, 0)), "strip",
         scratch=[pltpu.VMEM((cd * TILE, 2 * TILE), F32)],
     )
+    vm = IN_VMEM
     piece = pl.pallas_call(
-        solve_kernel, out_shape=jax.ShapeDtypeStruct(strip_part.shape[1:], jnp.int16), name="solve"
-    )(scatter(strip_part), inverse)
+        solve_kernel, out_shape=jax.ShapeDtypeStruct(pieces[2:], jnp.int16), name="solve",
+        in_specs=[smem, smem, vm, vm, vm], out_specs=vm,
+    )(pos, parent_place, scatter(strip_part), diagonal, inverse)
     wc, wr = spread(piece)
 
-    rr = jnp.broadcast_to(my_rows[:, :, None], (2, rd, cd))
-    cc = jnp.broadcast_to(my_cols[:, None, :], (2, rd, cd))
-    ok = (rr >= 0) & (cc >= 0)
-    send_row = jnp.maximum(rr, 0) // td
-    from_b = jnp.maximum(cc, 0) // td
-    same = from_b // wide == core
-    send = jnp.arange(2, dtype=i32)[:, None, None] * rown + send_row
-    from_b = from_b % wide
-    lists = []
-    for c in range(2):
-        for kind in (same, ~same):
-            flag = ok[c] & kind[c]
-            lists.append((jnp.where(flag, send[c], 0), jnp.where(flag, from_b[c], 0), flag.astype(i32)))
-    here = col * cd + jnp.arange(cd, dtype=i32)
-    panel = jnp.where(here == e[0], 1, jnp.where(here == e[1], 2, 0))
-    rows = [x[n] for n in (0, 1) for x in lists] + [x[2] for x in lists]
-    rows.append(jnp.broadcast_to(panel, (rd, cd)))
-    table = jnp.stack(rows).reshape(13, rd * cd)
-
-    def from_list(n):
-        return pl.BlockSpec(
-            (1, CODED, TILE), lambda i, j, t: (t[n, i * cd + j], 0, t[4 + n, i * cd + j])
-        )
-
+    per = 2
     return tile_call(
-        final_kernel, (rd, cd), (table,), (parent_front, first, second, first, second, wr, wc),
-        [pl.BlockSpec((TILE, TILE), lambda i, j, t: (i, j))] + [from_list(n) for n in range(4)] + [
+        final_kernel, (rd, cd // per), (fint,), (parent_front, first, second, wr, wc),
+        [
+            pl.BlockSpec((TILE, per * TILE), lambda i, j, t: (i, j)),
+            pl.BlockSpec(first.shape, lambda i, j, t: (0, 0, 0)),
+            pl.BlockSpec(second.shape, lambda i, j, t: (0, 0, 0)),
             pl.BlockSpec(wr.shape, lambda i, j, t: (0, 0, 0)),
             pl.BlockSpec(wc.shape, lambda i, j, t: (0, 0, 0)),
         ],
         jax.ShapeDtypeStruct(parent_front.shape, F32),
-        pl.BlockSpec((TILE, TILE), lambda i, j, t: (i, j)), "final",
+        pl.BlockSpec((TILE, per * TILE), lambda i, j, t: (i, j)), "final",
         scratch=[pltpu.VMEM((n * TILE, 2 * TILE), BF16) for n in (rd, rd, cd, cd)],
     )
 

time: 268 us -> 200 us (0.75)
  Pallas kernels: 214 us -> 187 us
  waiting for transfers between devices: 20.9 us -> 0.01 us
  local copies, waits for them, and re-layouts: 12.8 us -> 1.99 us
  other arithmetic: 6.85 us -> 0 us
    all_to_all x1, waiting for transfers between devices: 20.9 us -> 0.01 us  [body(): lax.all_to_all(outgoing, 'col', split_axis=0, concat_axis=0, tiled=True)]
    pallas_call x4, Pallas kernels: 119 us -> 104 us  [remote_call(): pl.pallas_call(kernel, out_shape=out_shape, in_specs=[pl.BlockSpec(memory...]
    pallas_call x5, Pallas kernels: 61.9 us -> 47.6 us  [tile_call(): pl.pallas_call(kernel, grid_spec=pltpu.PrefetchScalarGridSpec(num_scalar_...]
    gather x10 -> x0, local copies, waits for them, and re-layouts: 5.13 us -> none  [the longest x4 2.56 us: body(): ia, ib, ea, eb = (ie[pair_a], ie[pair_b], e[pair_a], e[pair_b])]
    select_n x12 -> x0, other arithmetic: 3.58 us -> none  [the longest x1 1.94 us: body(): part = jnp.where(row_ok[col] != 0, part, jnp.zeros_like(part))]
    pallas_call x1 -> x2, Pallas kernels: 4.22 us -> 7.55 us  [the longest x1 4.05 us: body(): pl.pallas_call(solve_kernel, out_shape=jax.ShapeDtypeStruct(pieces[2:], j...]
    another operation x17 -> x1, local copies, waits for them, and re-layouts: 3.51 us -> 0.63 us  [body(): pos = jnp.stack([ci, row, col, core, me, col * cd]).astype(i32)]
  transfers between devices with their start and end apart: 3 -> 3, of which waited for: 1 -> 0; matrix products, arithmetic and copies ran while one was open for 5% -> 0% of each run, Pallas kernels for 63% -> 77%
where the time goes in v2:
time: 200 us; the launch traced here: 197 us
  Pallas kernels  187 us (94%)
  starting transfers between devices  8.29 us (4%)
    pallas_call x4, Pallas kernels, remote_call(): pl.pallas_call(kernel, out_shape=out_shape, in_specs=[pl.BlockSpec(memory...  104 us
    pallas_call x5, Pallas kernels, tile_call(): pl.pallas_call(kernel, grid_spec=pltpu.PrefetchScalarGridSpec(num_scalar_...  47.6 us
    pallas_call x1, Pallas kernels, factor_inverse(): pl.pallas_call(factor_kernel, out_shape=jax.ShapeDtypeStruct(d.shape, F32...  28.2 us
    all_to_all x1, starting transfers between devices, body(): lax.all_to_all(outgoing, 'col', split_axis=0, concat_axis=0, tiled=True)  4.53 us
    pallas_call x1, Pallas kernels, body(): pl.pallas_call(solve_kernel, out_shape=jax.ShapeDtypeStruct(pieces[2:], j...  4.05 us
  transfers between devices with their start and end apart: 3, of which 0 were waited for; matrix products, arithmetic and copies ran while one was open for 0% of the time, Pallas kernels for 77%

profile of v2, /device:TPU:25, one launch (start us, length us, event | category | flops | bytes accessed | tf_op | source)
XLA Modules:
  0.0 197.2 jit_solution(13080584438771282451)
XLA Ops:
  0.0 0.6 stack.27.pos
  0.6 6.2 %pick.1 = (s16[4,4,272,256]{3,2,1,0:T(8,128)(2,1)}, bf16[256,1024]{1,0:T(8,128)(2,1)}) custom-call(s32[6]{0:T(128)} %stack.27.pos, s32[2,16]{1,0:T(2,128)} %maps.3, s32[24]{0:T(128)} %place.5, f32[1024,1024]{1,0:T(8,128)} %bitcast.14, bf16[1024,1024]{1,0:T(8,128)(2,1)} %bitcast.11), custom_call_target="tpu_custom_call" | custom-call | tf_op jit(solution)/shard_map/pick/pallas_call | solution.py:31
  6.8 4.5 %all-to-all-start = ((s16[4,4,272,256]{3,2,1,0:T(8,128)(2,1)}), s16[4,4,272,256]{3,2,1,0:T(8,128)(2,1)S(1)}, u32[]{:S(2)}, u32[]{:S(2)}) async-start(s16[4,4,272,256]{3,2,1,0:T(8,128)(2,1)} %get-tuple-element.26), calls=%async_computation | async-start | bytes 4456448 | tf_op jit(solution)/shard_map/all_to_all | solution.py:683
  11.3 3.5 %plan.1 = (s32[6]{0:T(128)}, s32[4,4]{1,0:T(4,128)}, s32[8,4]{1,0:T(8,128)}, s32[7,6]{1,0:T(8,128)}, s32[7,18]{1,0:T(8,128)}) custom-call(s32[6]{0:T(128)} %stack.27.pos, s32[2,16]{1,0:T(2,128)} %maps.3, s32[24]{0:T(128)} %place.5, s32[2,16,16]{2,1,0:T(8,128)} %pat.1), custom_call_target="tpu_custom_call" | custom-call | tf_op jit(solution)/shard_map/plan/pallas_call | solution.py:688
  14.8 18.3 %panels.1.eb.partner = bf16[4,256,1024]{2,1,0:T(8,128)(2,1)} custom-call(bf16[256,1024]{1,0:T(8,128)(2,1)} %get-tuple-element.25.x), custom_call_target="tpu_custom_call" | custom-call | bytes 1048576 | tf_op jit(solution)/shard_map/panels/pallas_call | solution.py:312
  33.1 5.4 %diag.1 = f32[512,512]{1,0:T(8,128)} custom-call(s32[8,4]{1,0:T(8,128)} %get-tuple-element.24.t, f32[1024,1024]{1,0:T(8,128)} %bitcast.15, f32[768,1536]{1,0:T(8,128)} %front.3, bf16[1024,1024]{1,0:T(8,128)(2,1)} %bitcast.12, bf16[4,256,1024]{2,1,0:T(8,128)(2,1)} %panels.1.eb.partner), custom_call_target="tpu_custom_call" | custom-call | tf_op jit(solution)/shard_map/diag/pallas_call | solution.py:31
  38.6 38.9 %total.1 = f32[2,4,4,16,512]{4,3,2,1,0:T(8,128)} custom-call(f32[2,4,4,16,512]{4,3,2,1,0:T(8,128)} %bitcast.18), custom_call_target="tpu_custom_call" | custom-call | bytes 1048576 | tf_op jit(solution)/shard_map/total/pallas_call | solution.py:312
  77.5 0.0 all-to-all-done.raw
  77.5 0.0 copy-start.1
  77.5 1.4 copy-done.1
  78.8 13.5 %update.1 = (f32[2,256,1024]{2,1,0:T(8,128)}, s16[4,2,272,512]{3,2,1,0:T(8,128)(2,1)}) custom-call(s32[6]{0:T(128)} %get-tuple-element.22.rowt, s32[4,4]{1,0:T(4,128)} %get-tuple-element.23.fac, s16[4,4,272,256]{3,2,1,0:T(8,128)(2,1)} %copy-done.1, bf16[1024,1024]{1,0:T(8,128)(2,1)} %bitcast.13, bf16[4,256,1024]{2,1,0:T(8,128)(2,1)} %panels.1.eb.partner), custom_call_target="tpu_custom_call" | custom-call | tf_op jit(solution)/shard_map/update/pallas_call | solution.py:31
  92.3 3.7 %all-to-all-start.1 = ((s16[8,272,512]{2,1,0:T(8,128)(2,1)}), s16[8,272,512]{2,1,0:T(8,128)(2,1)S(1)}, u32[]{:S(2)}, u32[]{:S(2)}) async-start(s16[8,272,512]{2,1,0:T(8,128)(2,1)} %bitcast.19), calls=%async_computation.1 | async-start | bytes 4456448 | tf_op jit(solution)/shard_map/all_to_all | solution.py:728
  95.9 28.2 %factor.1.inverse = f32[512,512]{1,0:T(8,128)} custom-call(f32[512,512]{1,0:T(8,128)} %bitcast.16), custom_call_target="tpu_custom_call" | custom-call | flops 40000000000 | bytes 2097152 | tf_op jit(solution)/shard_map/factor/pallas_call | solution.py:628
  124.1 0.0 all-to-all-done.1.first
  124.1 0.0 copy-start
  124.1 0.1 collective-permute-start
  124.2 7.5 %strip.1.x = s16[2,4,208,512]{3,2,1,0:T(8,128)(2,1)} custom-call(s32[7,6]{1,0:T(8,128)} %get-tuple-element.32.t, f32[2,256,1024]{2,1,0:T(8,128)} %get-tuple-element.33.upd, f32[768,1536]{1,0:T(8,128)} %front.3, f32[768,1536]{1,0:T(8,128)} %front.3), custom_call_target="tpu_custom_call" | custom-call | tf_op jit(solution)/shard_map/strip/pallas_call | solution.py:31
  131.8 0.0 copy-done
  131.8 16.1 %strips.1.parts = s16[4,208,512]{2,1,0:T(8,128)(2,1)} custom-call(s16[2,4,208,512]{3,2,1,0:T(8,128)(2,1)} %strip.1.x), custom_call_target="tpu_custom_call" | custom-call | bytes 1048576 | tf_op jit(solution)/shard_map/strips/pallas_call | solution.py:312
  147.9 4.1 %solve.1.x = s16[208,512]{1,0:T(8,128)(2,1)} custom-call(s32[6]{0:T(128)} %stack.27.pos, s32[24]{0:T(128)} %place.5, s16[4,208,512]{2,1,0:T(8,128)(2,1)} %strips.1.parts, f32[512,512]{1,0:T(8,128)} %bitcast.17, f32[512,512]{1,0:T(8,128)} %factor.1.inverse), custom_call_target="tpu_custom_call" | custom-call | tf_op jit(solution)/shard_map/solve/pallas_call | solution.py:747
  152.0 30.2 %spread.1 = (s16[8,208,512]{2,1,0:T(8,128)(2,1)}, s16[4,208,512]{2,1,0:T(8,128)(2,1)}) custom-call(s16[208,512]{1,0:T(8,128)(2,1)} %solve.1.x), custom_call_target="tpu_custom_call" | custom-call | bytes 1048576 | tf_op jit(solution)/shard_map/spread/pallas_call | solution.py:312
  182.2 0.0 collective-permute-done.second
  182.2 15.0 %final.1 = f32[768,1536]{1,0:T(8,128)} custom-call(s32[7,18]{1,0:T(8,128)} %get-tuple-element.21.t, f32[768,1536]{1,0:T(8,128)} %front.3, s16[8,272,512]{2,1,0:T(8,128)(2,1)} %copy-done, s16[8,272,512]{2,1,0:T(8,128)(2,1)} %collective-permute-done.second, s16[4,208,512]{2,1,0:T(8,128)(2,1)} %get-tuple-element.35.wr, s16[8,208,512]{2,1,0:T(8,128)(2,1)} %get-tuple-element.36.wc), custom_call_target="tpu_custom_call" | custom-call | tf_op jit(solution)/shard_map/final/pallas_call | solution.py:31
Async XLA Ops:
  6.8 70.7 %all-to-all-start = ((s16[4,4,272,256]{3,2,1,0:T(8,128)(2,1)}), s16[4,4,272,256]{3,2,1,0:T(8,128)(2,1)S(1)}, u32[]{:S(2)}, u32[]{:S(2)}) async-start(s16[4,4,272,256]{3,2,1,0:T(8,128)(2,1)} %get-tuple-element.26), calls=%async_computation | async-start | bytes 4456448 | tf_op jit(solution)/shard_map/all_to_all | solution.py:683
  77.5 1.4 copy-start.1
  92.3 31.8 %all-to-all-start.1 = ((s16[8,272,512]{2,1,0:T(8,128)(2,1)}), s16[8,272,512]{2,1,0:T(8,128)(2,1)S(1)}, u32[]{:S(2)}, u32[]{:S(2)}) async-start(s16[8,272,512]{2,1,0:T(8,128)(2,1)} %bitcast.19), calls=%async_computation.1 | async-start | bytes 4456448 | tf_op jit(solution)/shard_map/all_to_all | solution.py:728
  124.1 7.6 %copy-start = (s16[8,272,512]{2,1,0:T(8,128)(2,1)}, s16[8,272,512]{2,1,0:T(8,128)(2,1)S(1)}, u32[]{:S(2)}) copy-start(s16[8,272,512]{2,1,0:T(8,128)(2,1)S(1)} %all-to-all-done.1.first) | copy-start | bytes 6684676
  124.1 58.1 %collective-permute-start = (s16[8,272,512]{2,1,0:T(8,128)(2,1)S(1)}, s16[8,272,512]{2,1,0:T(8,128)(2,1)}, u32[]{:S(2)}, u32[]{:S(2)}) collective-permute-start(s16[8,272,512]{2,1,0:T(8,128)(2,1)S(1)} %all-to-all-done.1.first), channel_id=1, source_target_pairs={{0,4},{4,0},{1,5},{5,1},{2,6},{6,2},{3,7},{7,3},{8,12},{12,8},{9,1... | collective-permute-start | bytes 6684680 | tf_op jit(solution)/shard_map/ppermute | solution.py:732

commit v3 on v2

--- a/solution.py
+++ b/solution.py
@@ -15,7 +15,6 @@
 CODED = TILE + META
 FULL = 32767.0
 NT = (((1,), (1,)), ((), ()))
-NN = (((1,), (0,)), ((), ()))
 
 
 def dot(a, b, dims):
@@ -27,7 +26,7 @@
     return hi, (x - hi.astype(F32)).astype(BF16)
 
 
-def tile_call(kernel, grid, tables, operands, in_specs, out_shape, out_spec, name, cost=None, scratch=()):
+def tile_call(kernel, grid, tables, operands, in_specs, out_shape, out_spec, cost=None, scratch=()):
     return pl.pallas_call(
         kernel,
         grid_spec=pltpu.PrefetchScalarGridSpec(
@@ -35,7 +34,6 @@
             scratch_shapes=list(scratch),
         ),
         out_shape=out_shape,
-        name=name,
         cost_estimate=cost,
     )(*tables, *operands)
 
@@ -75,14 +73,20 @@
     return at, ok
 
 
-def pick_kernel(td, cd, pos, maps, place, src, panel, out, part):
-    n = out.shape[1]
-    for r in range(n):
+def pick_kernel(td, cd, pos, maps, place, src, panel, *outs):
+    part, tmp = outs[-2:]
+    z = pl.program_id(0)
+    for r in range(td):
         q, meta = encode(src[r * TILE : (r + 1) * TILE, :])
-        out[0, r, :TILE, :] = q
-        out[0, r, TILE:, :] = meta
-
-    @pl.when(pl.program_id(0) == 0)
+        tmp[r, :TILE, :] = q
+        tmp[r, TILE:, :] = meta
+    for d, out in enumerate(outs[:-2]):
+
+        @pl.when(z == d)
+        def _(out=out):
+            out[...] = tmp[...]
+
+    @pl.when(z == 0)
     def _():
         ok = find(maps, place, pos[0], pos[1], pos[2], td, cd)[1]
         part[...] = jnp.where(ok != 0, panel[...], jnp.zeros_like(panel))
@@ -92,7 +96,8 @@
     td, cd, rd, chips, blocks, cores, rown = dims
     ci, row, col, core = pos[0], pos[1], pos[2], pos[3]
     group = ci * rown + row
-    wide = blocks // cores
+    chip = pos[6]
+    rxn = chips // 2
     slots_n, tiles_n = place.shape[0], maps.shape[1]
 
     @pl.loop(0, slots_n)
@@ -105,20 +110,21 @@
         inv[0, place[maps[0, k]]] = k
         inv[1, place[maps[1, k]]] = k
 
-    cols = [find(maps, place, ci, b, col, td, cd) for b in range(blocks)]
-    for x in range(chips):
-        at, ok = find(maps, place, ci, row, x, td, cd)
-        rowt[x] = at
-        for b, (tile, good) in enumerate(cols):
-            fac[x, b] = pat[ci, row * td + at, b * td + tile] * ok * good
+    from_col = [lax.rem(col + blocks - d, blocks) for d in range(blocks)]
+    cols = [find(maps, place, ci, b, col, td, cd) for b in from_col]
+    for d in range(chips):
+        at, ok = find(maps, place, ci, row, lax.rem(chip + d, chips), td, cd)
+        rowt[d] = at
+        for n, (b, (tile, good)) in enumerate(zip(from_col, cols)):
+            fac[d, n] = pat[ci, row * td + at, b * td + tile] * ok * good
     e = (place[0], place[1])
     ie = (inv[ci, e[0]], inv[ci, e[1]])
     le = [jnp.maximum(i, 0) for i in ie]
     own = [((ie[a] >= 0) & (le[a] // td == row)).astype(jnp.int32) for a in range(2)]
     for a in range(2):
-        rowt[chips + a] = jnp.where(own[a] != 0, e[a] // cd, -1)
-        for b in range(2):
-            k = a * 2 + b
+        rowt[chips + a] = jnp.where(own[a] != 0, lax.rem(e[a] // cd + chips - chip, chips), -1)
+        for b in range(a + 1):
+            k = a + b
             live = own[a] * (ie[b] >= 0).astype(jnp.int32) * pat[ci, le[a], le[b]]
             diagt[0, k] = le[a] % td
             diagt[1, k] = le[b] % td
@@ -146,51 +152,60 @@
         for c in range(2):
             r, t = inv[c, group * rd + k // cd], inv[c, slot]
             ok = ((r >= 0) & (t >= 0)).astype(jnp.int32)
-            b = jnp.maximum(t, 0) // td
-            same = (b // wide == core).astype(jnp.int32)
-            fint[3 * c, k] = c * rown + jnp.maximum(r, 0) // td
-            fint[3 * c + 1, k] = b % wide
-            fint[3 * c + 2, k] = ok * (2 - same)
+            source = jnp.maximum(r, 0) // td
+            far = (source % cores != core).astype(jnp.int32)
+            fint[3 * c, k] = far * chips + lax.rem(chip + chips - (c * rxn + source // cores), chips)
+            fint[3 * c + 1, k] = jnp.maximum(t, 0) // td
+            fint[3 * c + 2, k] = ok
         fint[6, k] = jnp.where(slot == e[0], 1, jnp.where(slot == e[1], 2, 0))
 
 
 def diag_kernel(t, blk, front, ea, eb, out):
-    k = pl.program_id(0) * 2 + pl.program_id(1)
+    k = pl.program_id(0)
     x = jnp.where(t[4, k] != 0, blk[...], 0.0) + jnp.where(t[5, k] != 0, front[...], 0.0)
     out[...] = x - jnp.where(t[6, k] != 0, dot(ea[...], eb[0], NT), 0.0)
 
 
-def update_kernel(rowt, fac, raw, panel, partner, strip, coded):
+def update_kernel(rowt, fac, pos, *refs):
+    blocks = fac.shape[1]
+    raws, (panel, partner, strip), outs, tmp = refs[:blocks], refs[blocks : blocks + 3], refs[blocks + 3 : -1], refs[-1]
     p = pl.program_id(0)
     chips = pl.num_programs(0)
-    blocks = partner.shape[0]
-    wide = coded.shape[3] // TILE
 
     @pl.when(p == 0)
     def _():
         strip[...] = jnp.zeros_like(strip)
 
-    for b in range(blocks):
-        u = decode(raw[b, 0]) - dot(panel[...], partner[b], NT)
-        u = jnp.where(fac[p, b] != 0, u, 0.0)
-        at = slice(b % wide * TILE, (b % wide + 1) * TILE)
+    for d, raw in enumerate(raws):
+        b = lax.rem(pos[2] + blocks - d, blocks)
+        at = pl.ds(pl.multiple_of(b * TILE, TILE), TILE)
+        u = decode(raw[0]) - dot(panel[...], partner[b], NT)
+        u = jnp.where(fac[p, d] != 0, u, 0.0)
         q, meta = encode(u)
-        coded[0, b // wide, :TILE, at] = q
-        coded[0, b // wide, TILE:, at] = meta
+        tmp[:TILE, at] = q
+        tmp[TILE:, at] = meta
         for a in range(2):
 
             @pl.when(rowt[chips + a] == p)
-            def _(a=a, u=u, b=b):
-                strip[a, :, b * TILE : (b + 1) * TILE] = u
-
-
-def strip_kernel(t, upd, f0, f1, out, g):
+            def _(a=a, u=u, at=at):
+                strip[a, :, at] = u
+
+    for d, out in enumerate(outs):
+
+        @pl.when(p == d)
+        def _(out=out):
+            out[...] = tmp[...]
+
+
+def strip_kernel(t, pos, upd, f0, f1, *outs):
+    g, outs = outs[-1], outs[:-1]
     cd = t.shape[1]
     some = sum(t[n, q] for n in range(3, 7) for q in range(cd))
 
     @pl.when(some == 0)
     def _():
-        out[...] = jnp.zeros_like(out)
+        for out in outs:
+            out[...] = jnp.zeros_like(out)
 
     @pl.when(some != 0)
     def _():
@@ -205,20 +220,20 @@
                     x = x + jnp.where(t[5 + a, q] != 0, f[:, q * TILE : (q + 1) * TILE], 0.0)
                     g[q * TILE : (q + 1) * TILE, a * TILE : (a + 1) * TILE] = x.T
 
-        n = out.shape[2] - META
-        for p in range(out.shape[1]):
-            for k in range(out.shape[0]):
-                m = p * out.shape[0] + k
-                code, meta = encode(g[m * n : (m + 1) * n, :])
-                out[k, p, :n, :] = code
-                out[k, p, n:, :] = meta
-
-
-def solve_kernel(pos, place, parts, diagonal, inverse, out):
+        n = outs[0].shape[0] - META
+        for d, out in enumerate(outs):
+            m = lax.rem(pos[4] + d, len(outs))
+            code, meta = encode(g[pl.ds(pl.multiple_of(m * n, 16), n), :])
+            out[:n, :] = code
+            out[n:, :] = meta
+
+
+def solve_kernel(pos, place, diagonal, inverse, *refs):
+    out = refs[-1]
     n = out.shape[0] - META
-    g = decode(parts[0])
-    for p in range(1, parts.shape[0]):
-        g = g + decode(parts[p])
+    g = decode(refs[0][...])
+    for part in refs[1:-1]:
+        g = g + decode(part[...])
     unit = math.gcd(n, TILE)
     rows = []
     for u in range(n // unit):
@@ -236,18 +251,25 @@
     out[n:, :] = meta
 
 
-def final_kernel(t, front, first, second, wr, wc, out, rh, rl, ch, cl):
+def final_kernel(t, front, wr, wc, *refs):
+    out, rh, rl, ch, cl, buf, sem = refs[-7:]
+    codes = refs[:-7]
     i, j = pl.program_id(0), pl.program_id(1)
     per = out.shape[1] // TILE
     base = (i * pl.num_programs(1) + j) * per
 
     @pl.when(base == 0)
     def _():
+        cps = [pltpu.make_async_copy(x, buf.at[n], sem.at[n]) for n, x in enumerate(codes)]
+        for cp in cps:
+            cp.start()
         for src, hi, lo in ((wr, rh, rl), (wc, ch, cl)):
             n = src.shape[1] - META
             for p in range(src.shape[0]):
                 at = pl.ds(p * n, n)
                 hi[at, :], lo[at, :] = split(decode(src[p]))
+        for cp in cps:
+            cp.wait()
 
     ri = pl.ds(pl.multiple_of(i * TILE, TILE), TILE)
     cj = pl.ds(pl.multiple_of(j * TILE * per, TILE), TILE * per)
@@ -258,12 +280,11 @@
         k = base + m
         at = slice(m * TILE, (m + 1) * TILE)
         for c in range(2):
-            for n, src in enumerate((first, second)):
-
-                @pl.when(t[3 * c + 2, k] == n + 1)
-                def _(src=src, c=c, k=k, at=at):
-                    lanes = pl.ds(pl.multiple_of(t[3 * c + 1, k] * TILE, TILE), TILE)
-                    out[:, at] = out[:, at] + decode(src[t[3 * c, k], :, lanes])
+
+            @pl.when(t[3 * c + 2, k] != 0)
+            def _(c=c, k=k, at=at):
+                lanes = pl.ds(pl.multiple_of(t[3 * c + 1, k] * TILE, TILE), TILE)
+                out[:, at] = out[:, at] + decode(buf[t[3 * c, k], :, lanes])
 
         for n in range(2):
 
@@ -308,7 +329,7 @@
     return cp
 
 
-def remote_call(kernel, operands, out_shape, out_specs, scratch, cid, name, flops=0):
+def remote_call(kernel, operands, out_shape, out_specs, scratch, cid, flops=0):
     return pl.pallas_call(
         kernel,
         out_shape=out_shape,
@@ -317,7 +338,6 @@
         scratch_shapes=scratch,
         compiler_params=pltpu.CompilerParams(collective_id=cid, has_side_effects=True),
         cost_estimate=pl.CostEstimate(flops=flops, bytes_accessed=1 << 20, transcendentals=0),
-        name=name,
     )(*operands)
 
 
@@ -352,7 +372,7 @@
     dma = pltpu.SemaphoreType.DMA
     return remote_call(
         panel_kernel, (x,), jax.ShapeDtypeStruct(shape, x.dtype), ANY,
-        [dma, dma((n,)), dma((n,)), dma((n,)), dma((n,))], 0, "panels",
+        [dma, dma((n,)), dma((n,)), dma((n,)), dma((n,))], 0,
     )
 
 
@@ -379,66 +399,48 @@
     for d in range(nz - 1):
         total = total + zgot[d]
     out[s.core, s.chip, s.col] = total
-    own = out.at[s.core, s.chip, s.col]
-    cps = [push(own, own, ss3.at[d], rs3.at[d], {"col": t}) for d, t in enumerate(cols)]
-    for cp in cps:
+
+    def send_z(d, t):
+        own = out.at[s.core, s.chip, s.col]
+        return push(own, own, ss3.at[d], rs3.at[d], {"col": t})
+
+    def send_xy(z, n):
+        own = out.at[s.core, s.chip, z]
+        return [push(own, own, ss4.at[n, d], rs4.at[n, d], s.id(t)) for d, t in enumerate(chips)]
+
+    def send_core(c, z, n, m):
+        own = out.at[s.core, c, z]
+        return push(own, own, ss5.at[n, m], rs5.at[n, m], s.other)
+
+    zc = [send_z(d, t) for d, t in enumerate(cols)]
+    xy = [send_xy(s.col, 0)]
+    cc = [send_core(s.chip, s.col, 0, 0)]
+    for n in range(nz):
+        z = s.turn(s.col, -n, nz)
+        if n:
+            zc[n - 1].wait_recv()
+            xy.append(send_xy(z, n))
+            cc.append(send_core(s.chip, z, n, 0))
+    for n in range(nz):
+        for d in range(nc - 1):
+            xy[n][d].wait_recv()
+            cc.append(send_core(s.turn(s.chip, -(d + 1), nc), s.turn(s.col, -n, nz), n, d + 1))
+    for cp in zc + [x for row in xy for x in row]:
+        cp.wait_send()
+    for cp in cc:
         cp.wait()
-    own = out.at[s.core, s.chip]
-    cps = [push(own, own, ss4.at[d], rs4.at[d], s.id(t)) for d, t in enumerate(chips)]
-    for cp in cps:
-        cp.wait()
-    own = out.at[s.core]
-    push(own, own, ss5, rs5, s.other).wait()
 
 
 def sum_all(x):
-    n = x.shape[0]
     nc, nz = lax.axis_size(("child", "rx")), lax.axis_size("col")
-    tail = (n // (2 * nc * nz), n)
+    tail = (x.shape[0] // (2 * nc * nz), x.shape[1])
     full = jax.ShapeDtypeStruct((2, nc, nz) + tail, F32)
     dma = pltpu.SemaphoreType.DMA
-    sems = [dma, dma, dma((nc,)), dma((nc,)), dma((nz,)), dma((nz,)), dma((nz,)), dma((nz,)), dma((nc,)), dma((nc,)), dma, dma]
+    sems = [dma, dma, dma((nc,)), dma((nc,)), dma((nz,)), dma((nz,)), dma((nz,)), dma((nz,)), dma((nz, nc)), dma((nz, nc)), dma((nz, nc)), dma((nz, nc))]
     half, part = (nc, nz) + tail, (nz,) + tail
     vm = [pltpu.VMEM(z, F32) for z in (half, half, (nc - 1,) + part, part, (nz - 1,) + tail)]
-    out = remote_call(sum_kernel, (x.reshape(full.shape),), full, IN_VMEM, vm + sems, 1, "total")
-    return out.reshape(n, n)
-
-
-def scatter_kernel(x, out, half, mine, ss, rs, cs, cr):
-    s = Spot()
-    nc = s.chips
-    n = x.shape[2] - META
-    order = [s.turn(s.chip, d, nc) for d in range(1, nc + 1)]
-    greet([s.other] + [s.id(t) for t in order[:-1]])
-    pairs = [push(x.at[1 - s.core, t], half.at[t], ss.at[d], rs.at[t], s.other) for d, t in enumerate(order)]
-    cps = []
-    for d, t in enumerate(order):
-        pltpu.make_async_remote_copy(
-            src_ref=half.at[t], dst_ref=half.at[t], send_sem=ss.at[d], recv_sem=rs.at[t],
-            device_id=s.other, device_id_type=MESH,
-        ).wait_recv()
-        q, meta = encode(decode(x[s.core, t]) + decode(half[t]))
-        if d < nc - 1:
-            mine[d, :n, :] = q
-            mine[d, n:, :] = meta
-            cps.append(push(mine.at[d], out.at[d + 1], cs.at[d], cr.at[d], s.id(t)))
-        else:
-            out[0, :n, :] = q
-            out[0, n:, :] = meta
-    for cp in pairs:
-        cp.wait_send()
-    for cp in cps:
-        cp.wait()
-
-
-def scatter(x):
-    nc = x.shape[1]
-    dma = pltpu.SemaphoreType.DMA
-    shape = x.shape[1:]
-    return remote_call(
-        scatter_kernel, (x,), jax.ShapeDtypeStruct(shape, x.dtype), IN_VMEM,
-        [pltpu.VMEM(shape, x.dtype)] * 2 + [dma((nc,))] * 4, 2, "strips"
-    )
+    out = remote_call(sum_kernel, (x.reshape(full.shape),), full, IN_VMEM, vm + sems, 1)
+    return out.reshape(x.shape)
 
 
 def spread_kernel(x, wc, wr, zbuf, loc, zs, zr, ps, pr, fs, fr, ws, wx, wl):
@@ -559,9 +561,7 @@
     dma = pltpu.SemaphoreType.DMA
     sems = [dma, dma((2 * nz,)), dma((nz,))] + [dma((nc,))] * 4 + [dma((2 * nz,)), dma((nc,)), dma]
     shapes = [jax.ShapeDtypeStruct((n,) + x.shape, x.dtype) for n in (2 * nc, nc)]
-    return remote_call(
-        spread_kernel, (x,), shapes, [ANY, ANY], [pltpu.VMEM((nz,) + x.shape, x.dtype)] + sems, 3, "spread"
-    )
+    return remote_call(spread_kernel, (x,), shapes, [ANY, ANY], [pltpu.VMEM((nz,) + x.shape, x.dtype)] + sems, 3)
 
 
 BASE = 128
@@ -601,11 +601,15 @@
         x_ref[i * step : (i + 1) * step, :] = x[i] * (1.0 / jnp.sqrt(d_ref[i * step : (i + 1) * step, :]))
 
 
-def factor_kernel(a_in, y, a, blk, piv, inv):
+def factor_kernel(a_in, y, full, a, blk, piv, inv):
     n = a.shape[0]
     high = functools.partial(lax.dot_general, precision=lax.Precision.HIGHEST, preferred_element_type=F32)
     ids = lax.broadcasted_iota(jnp.int32, (n, n), 0)
-    a[...] = a_in[...]
+    a[:TILE, :TILE] = a_in[:TILE, :]
+    a[TILE:, :TILE] = a_in[TILE : 2 * TILE, :]
+    a[:TILE, TILE:] = a_in[TILE : 2 * TILE, :].T
+    a[TILE:, TILE:] = a_in[2 * TILE :, :]
+    full[...] = a[...]
     y[...] = (ids == lax.broadcasted_iota(jnp.int32, (n, n), 1)).astype(F32)
 
     def one(k, carry):
@@ -624,10 +628,10 @@
 
 
 def factor_inverse(d):
-    n = d.shape[0]
+    n = 2 * TILE
     return pl.pallas_call(
         factor_kernel,
-        out_shape=jax.ShapeDtypeStruct(d.shape, F32),
+        out_shape=[jax.ShapeDtypeStruct((n, n), F32)] * 2,
         scratch_shapes=[pltpu.VMEM((n, n), F32)] + [pltpu.VMEM((BASE, BASE), F32)] * 3,
         name="factor",
         cost_estimate=pl.CostEstimate(flops=FACTOR_WORK, bytes_accessed=8 * n * n, transcendentals=0),
@@ -645,7 +649,6 @@
     rown = rxn * cores
     chips = lax.axis_size("child") * rxn
     chip = ci * rxn + rx
-    group = ci * rown + row
     block = child_blocks[0]
     own = child_panels[0]
     depth = own.shape[1]
@@ -658,29 +661,31 @@
     i32 = jnp.int32
 
     share = cd * TILE // (chips * cores)
-    wide = blocks // cores
     me = chip * cores + core
-    pos = jnp.stack([ci, row, col, core, me, col * cd]).astype(i32)
+    pos = jnp.stack([ci, row, col, core, me, col * cd, chip]).astype(i32)
 
     def tile_at(block, group, pos, maps, place):
         return find(maps, place, pos[0], block, group, td, cd)[0]
 
-    outgoing, part = tile_call(
+    def shift(x, axes, d):
+        n = lax.axis_size(axes)
+        return lax.ppermute(x, axes, [(k, (k + d) % n) for k in range(n)])
+
+    code = (td, CODED, TILE)
+    *outgoing, part = tile_call(
         functools.partial(pick_kernel, td, cd), (blocks,), (pos, child_maps, parent_place), (block, own),
         [
-            pl.BlockSpec((width, TILE), lambda z, pos, maps, place: (0, tile_at(pos[2], z, pos, maps, place))),
+            pl.BlockSpec(
+                (width, TILE),
+                lambda z, pos, maps, place: (0, tile_at(pos[2], lax.rem(pos[2] + z, blocks), pos, maps, place)),
+            ),
             pl.BlockSpec((TILE, depth), lambda z, pos, maps, place: (tile_at(pos[1], pos[2], pos, maps, place), 0)),
         ],
-        [
-            jax.ShapeDtypeStruct((blocks, td, CODED, TILE), jnp.int16),
-            jax.ShapeDtypeStruct((TILE, depth), own.dtype),
-        ],
-        [
-            pl.BlockSpec((1, td, CODED, TILE), lambda z, *_: (z, 0, 0, 0)),
-            pl.BlockSpec((TILE, depth), lambda z, *_: (0, 0)),
-        ], "pick",
+        [jax.ShapeDtypeStruct(code, jnp.int16)] * blocks + [jax.ShapeDtypeStruct((TILE, depth), own.dtype)],
+        [pl.BlockSpec(code, lambda z, *_: (0, 0, 0))] * blocks + [pl.BlockSpec((TILE, depth), lambda z, *_: (0, 0))],
+        scratch=[pltpu.VMEM(code, jnp.int16)],
     )
-    raw = lax.all_to_all(outgoing, "col", split_axis=0, concat_axis=0, tiled=True)
+    raw = [shift(x, "col", d) if d else x for d, x in enumerate(outgoing)]
 
     smem = pl.BlockSpec(memory_space=pltpu.SMEM)
     dims = (td, cd, rd, chips, blocks, cores, rown)
@@ -694,75 +699,71 @@
 
     partner = panel_gather(part)
     diag_part = tile_call(
-        diag_kernel, (2, 2), (diagt,), (block, parent_front, own, partner),
+        diag_kernel, (3,), (diagt,), (block, parent_front, own, partner),
         [
-            pl.BlockSpec((TILE, TILE), lambda a, b, t: (t[0, a * 2 + b], t[1, a * 2 + b])),
-            pl.BlockSpec((TILE, TILE), lambda a, b, t: (t[2, a * 2 + b], t[3, a * 2 + b])),
-            pl.BlockSpec((TILE, depth), lambda a, b, t: (t[0, a * 2 + b], 0)),
-            pl.BlockSpec((1, TILE, depth), lambda a, b, t: (t[7, a * 2 + b], 0, 0)),
+            pl.BlockSpec((TILE, TILE), lambda k, t: (t[0, k], t[1, k])),
+            pl.BlockSpec((TILE, TILE), lambda k, t: (t[2, k], t[3, k])),
+            pl.BlockSpec((TILE, depth), lambda k, t: (t[0, k], 0)),
+            pl.BlockSpec((1, TILE, depth), lambda k, t: (t[7, k], 0, 0)),
         ],
-        jax.ShapeDtypeStruct((2 * TILE, 2 * TILE), F32),
-        pl.BlockSpec((TILE, TILE), lambda a, b, t: (a, b)), "diag",
+        jax.ShapeDtypeStruct((3 * TILE, TILE), F32),
+        pl.BlockSpec((TILE, TILE), lambda k, t: (k, 0)),
     )
     plane = ("child", "rx", "core")
     diagonal = sum_all(diag_part)
-    diagonal, raw = lax.optimization_barrier((diagonal, raw))
-
-    strip_rows, coded = tile_call(
-        update_kernel, (chips,), (rowt, fac), (raw, own, partner),
+    diagonal, *raw = lax.optimization_barrier((diagonal, *raw))
+
+    row_code = (CODED, blocks * TILE)
+    strip_rows, *coded = tile_call(
+        update_kernel, (chips,), (rowt, fac, pos), (*raw, own, partner),
+        [pl.BlockSpec((1, CODED, TILE), lambda p, r, f, pos: (r[p], 0, 0))] * blocks + [
+            pl.BlockSpec((TILE, depth), lambda p, r, f, pos: (r[p], 0)),
+            pl.BlockSpec((blocks, TILE, depth), lambda p, r, f, pos: (0, 0, 0)),
+        ],
+        [jax.ShapeDtypeStruct((2, TILE, blocks * TILE), F32)] + [jax.ShapeDtypeStruct(row_code, jnp.int16)] * chips,
+        [pl.BlockSpec((2, TILE, blocks * TILE), lambda p, *_: (0, 0, 0))]
+        + [pl.BlockSpec(row_code, lambda p, *_: (0, 0))] * chips,
+        scratch=[pltpu.VMEM(row_code, jnp.int16)],
+    )
+    piece = (share + META, 2 * TILE)
+    parts = tile_call(
+        strip_kernel, (1,), (stript, pos), (strip_rows, parent_front, parent_front),
         [
-            pl.BlockSpec((blocks, 1, CODED, TILE), lambda p, r, f: (0, r[p], 0, 0)),
-            pl.BlockSpec((TILE, depth), lambda p, r, f: (r[p], 0)),
-            pl.BlockSpec((blocks, TILE, depth), lambda p, r, f: (0, 0, 0)),
+            pl.BlockSpec(strip_rows.shape, lambda k, t, pos: (0, 0, 0)),
+            pl.BlockSpec((TILE, cd * TILE), lambda k, t, pos: (t[0, 0], 0)),
+            pl.BlockSpec((TILE, cd * TILE), lambda k, t, pos: (t[0, 1], 0)),
         ],
-        [
-            jax.ShapeDtypeStruct((2, TILE, blocks * TILE), F32),
-            jax.ShapeDtypeStruct((chips, cores, CODED, wide * TILE), jnp.int16),
-        ],
-        [
-            pl.BlockSpec((2, TILE, blocks * TILE), lambda p, r, f: (0, 0, 0)),
-            pl.BlockSpec((1, cores, CODED, wide * TILE), lambda p, r, f: (p, 0, 0, 0)),
-        ], "update",
-    )
-    coded = coded.reshape((chips * cores,) + coded.shape[2:])
-    first = lax.all_to_all(coded, plane, split_axis=0, concat_axis=0, tiled=True)
-    diagonal, coded = lax.optimization_barrier((diagonal, coded))
-    inverse = factor_inverse(diagonal)
-    first, inverse = lax.optimization_barrier((first, inverse))
-    second = lax.ppermute(first, "core", [(k, (k + 1) % 2) for k in range(2)])
-
-    pieces = (cores, chips, share + META, 2 * TILE)
-    strip_part = tile_call(
-        strip_kernel, (1,), (stript,), (strip_rows, parent_front, parent_front),
-        [
-            pl.BlockSpec(strip_rows.shape, lambda k, t: (0, 0, 0)),
-            pl.BlockSpec((TILE, cd * TILE), lambda k, t: (t[0, 0], 0)),
-            pl.BlockSpec((TILE, cd * TILE), lambda k, t: (t[0, 1], 0)),
-        ],
-        jax.ShapeDtypeStruct(pieces, jnp.int16),
-        pl.BlockSpec(pieces, lambda k, t: (0, 0, 0, 0)), "strip",
+        [jax.ShapeDtypeStruct(piece, jnp.int16)] * (chips * cores),
+        [pl.BlockSpec(piece, lambda k, t, pos: (0, 0))] * (chips * cores),
         scratch=[pltpu.VMEM((cd * TILE, 2 * TILE), F32)],
     )
+    diagonal, parts, coded = lax.optimization_barrier((diagonal, list(parts), coded))
+    parts = [shift(x, plane, d) if d else x for d, x in enumerate(parts)]
+    first = [shift(x, ("child", "rx"), d) if d else x for d, x in enumerate(coded)]
+    inverse, diagonal = factor_inverse(diagonal)
+    inverse, parts = lax.optimization_barrier((inverse, parts))
+
     vm = IN_VMEM
     piece = pl.pallas_call(
-        solve_kernel, out_shape=jax.ShapeDtypeStruct(pieces[2:], jnp.int16), name="solve",
-        in_specs=[smem, smem, vm, vm, vm], out_specs=vm,
-    )(pos, parent_place, scatter(strip_part), diagonal, inverse)
+        solve_kernel, out_shape=jax.ShapeDtypeStruct(piece, jnp.int16), name="solve",
+        in_specs=[smem, smem] + [vm] * (2 + len(parts)), out_specs=vm,
+    )(pos, parent_place, diagonal, inverse, *parts)
+    piece, first = lax.optimization_barrier((piece, first))
+    second = [shift(x, "core", 1) for x in first]
     wc, wr = spread(piece)
 
     per = 2
     return tile_call(
-        final_kernel, (rd, cd // per), (fint,), (parent_front, first, second, wr, wc),
+        final_kernel, (rd, cd // per), (fint,), (parent_front, wr, wc, *first, *second),
         [
             pl.BlockSpec((TILE, per * TILE), lambda i, j, t: (i, j)),
-            pl.BlockSpec(first.shape, lambda i, j, t: (0, 0, 0)),
-            pl.BlockSpec(second.shape, lambda i, j, t: (0, 0, 0)),
             pl.BlockSpec(wr.shape, lambda i, j, t: (0, 0, 0)),
             pl.BlockSpec(wc.shape, lambda i, j, t: (0, 0, 0)),
-        ],
+        ] + [ANY] * (2 * chips),
         jax.ShapeDtypeStruct(parent_front.shape, F32),
-        pl.BlockSpec((TILE, per * TILE), lambda i, j, t: (i, j)), "final",
-        scratch=[pltpu.VMEM((n * TILE, 2 * TILE), BF16) for n in (rd, rd, cd, cd)],
+        pl.BlockSpec((TILE, per * TILE), lambda i, j, t: (i, j)),
+        scratch=[pltpu.VMEM((n * TILE, 2 * TILE), BF16) for n in (rd, rd, cd, cd)]
+        + [pltpu.VMEM((2 * chips,) + row_code, jnp.int16), pltpu.SemaphoreType.DMA((2 * chips,))],
     )
 
 

time: 200 us -> 202 us (1.010)
  Pallas kernels: 187 us -> 168 us
  waiting for transfers between devices: 0.01 us -> 14.9 us
  starting transfers between devices: 8.29 us -> 14.4 us
    pallas_call x4 -> x3, Pallas kernels: 104 us -> 85.8 us  [remote_call(): pl.pallas_call(kernel, out_shape=out_shape, in_specs=[pl.BlockSpec(memory...]
    ppermute x1 -> x17, waiting for transfers between devices: 0.01 us -> 14.9 us  [shift(): return lax.ppermute(x, axes, [(k, (k + d) % n) for k in range(n)])]
    ppermute x1 -> x17, starting transfers between devices: 0.11 us -> 14.4 us  [shift(): return lax.ppermute(x, axes, [(k, (k + d) % n) for k in range(n)])]
    all_to_all x2 -> x0, starting transfers between devices: 8.18 us -> none  [the longest x1 4.53 us: body(): lax.all_to_all(outgoing, 'col', split_axis=0, concat_axis=0, tiled=True)]
    pallas_call x5, Pallas kernels: 47.6 us -> 45.4 us  [tile_call(): pl.pallas_call(kernel, grid_spec=pltpu.PrefetchScalarGridSpec(num_scalar_...]
  transfers between devices with their start and end apart: 3 -> 17, of which waited for: 0 -> 3; matrix products, arithmetic and copies ran while one was open for 0% -> 0% of each run, Pallas kernels for 77% -> 63%
where the time goes in v3:
time: 202 us; the launch traced here: 201 us
  Pallas kernels  168 us (83%)
  waiting for transfers between devices  14.9 us (7%)
  starting transfers between devices  14.4 us (7%)
  local copies, waits for them, and re-layouts  3.4 us (2%)
    pallas_call x3, Pallas kernels, remote_call(): pl.pallas_call(kernel, out_shape=out_shape, in_specs=[pl.BlockSpec(memory...  85.8 us
    pallas_call x5, Pallas kernels, tile_call(): pl.pallas_call(kernel, grid_spec=pltpu.PrefetchScalarGridSpec(num_scalar_...  45.4 us
    pallas_call x1, Pallas kernels, factor_inverse(): pl.pallas_call(factor_kernel, out_shape=[jax.ShapeDtypeStruct((n, n), F32...  28.1 us
    ppermute x17, waiting for transfers between devices, shift(): return lax.ppermute(x, axes, [(k, (k + d) % n) for k in range(n)])  14.9 us
    ppermute x17, starting transfers between devices, shift(): return lax.ppermute(x, axes, [(k, (k + d) % n) for k in range(n)])  14.4 us
    pallas_call x1, Pallas kernels, body(): pl.pallas_call(solve_kernel, out_shape=jax.ShapeDtypeStruct(piece, jnp.in...  4.53 us
  transfers between devices with their start and end apart: 17, of which 3 were waited for; matrix products, arithmetic and copies ran while one was open for 0% of the time, Pallas kernels for 63%

profile of v3, /device:TPU:25, one launch (start us, length us, event | category | flops | bytes accessed | tf_op | source)
XLA Modules:
  0.0 200.7 jit_solution(4389264783929202883)
XLA Ops:
  0.0 0.7 stack.31.pos
  0.7 6.8 %shard_map.64 = (s16[4,272,256]{2,1,0:T(8,128)(2,1)}, s16[4,272,256]{2,1,0:T(8,128)(2,1)}, s16[4,272,256]{2,1,0:T(8,128)(2,1)}, s16[4,272,256]{2,1,0:T(8,128)(2,1)}, bf16[256,1024]{1,0:T(8,128)(2,1)}) custom-call(s32[7]{0:T(128)} %stack.31.pos, s32[2,16]{1,0:T(2,128)} %maps.3, s32[24]{0:T(128)} %place.5, f32[1024,1024]{1,0:T(8,128)} %bitcast.14, ...), custom_call_target="tpu_custom_call" | custom-call | tf_op jit(solution)/shard_map/pallas_call | solution.py:30
  7.5 1.3 collective-permute-start.1
  8.8 0.2 collective-permute-start.2
  9.0 3.6 %plan.1 = (s32[6]{0:T(128)}, s32[4,4]{1,0:T(4,128)}, s32[8,4]{1,0:T(8,128)}, s32[7,6]{1,0:T(8,128)}, s32[7,18]{1,0:T(8,128)}) custom-call(s32[7]{0:T(128)} %stack.31.pos, s32[2,16]{1,0:T(2,128)} %maps.3, s32[24]{0:T(128)} %place.5, s32[2,16,16]{2,1,0:T(8,128)} %pat.1), custom_call_target="tpu_custom_call" | custom-call | tf_op jit(solution)/shard_map/plan/pallas_call | solution.py:693
  12.6 18.6 %shard_map.65.eb.refs_5_ = bf16[4,256,1024]{2,1,0:T(8,128)(2,1)} custom-call(bf16[256,1024]{1,0:T(8,128)(2,1)} %get-tuple-element.66.x), custom_call_target="tpu_custom_call" | custom-call | bytes 1048576 | tf_op jit(solution)/shard_map/pallas_call | solution.py:333
  31.2 4.8 %shard_map.66 = f32[768,256]{1,0:T(8,128)} custom-call(s32[8,4]{1,0:T(8,128)} %get-tuple-element.65.t, f32[1024,1024]{1,0:T(8,128)} %bitcast.15, f32[768,1536]{1,0:T(8,128)} %front.3, bf16[1024,1024]{1,0:T(8,128)(2,1)} %bitcast.12, bf16[4,256,1024]{2,1,0:T(8,128)(2,1)} %shard_map.65.eb.refs_5_), custom_call_target="tpu_custom_call" | custom-call | tf_op jit(solution)/shard_map/pallas_call | solution.py:30
  36.0 36.1 %shard_map.67 = f32[2,4,4,24,256]{4,3,2,1,0:T(8,128)} custom-call(f32[2,4,4,24,256]{4,3,2,1,0:T(8,128)} %bitcast.16), custom_call_target="tpu_custom_call" | custom-call | bytes 1048576 | tf_op jit(solution)/shard_map/pallas_call | solution.py:333
  72.3 0.8 copy-done.4
  73.0 0.2 copy-done.5
  73.4 14.8 %shard_map.68 = (f32[2,256,1024]{2,1,0:T(8,128)}, s16[272,1024]{1,0:T(8,128)(2,1)}, s16[272,1024]{1,0:T(8,128)(2,1)}, s16[272,1024]{1,0:T(8,128)(2,1)}, s16[272,1024]{1,0:T(8,128)(2,1)}) custom-call(s32[6]{0:T(128)} %get-tuple-element.73.rowt, s32[4,4]{1,0:T(4,128)} %get-tuple-element.74.fac, s32[7]{0:T(128)} %stack.31.pos, ...), custom_call_target="tpu_custom_call" | custom-call | tf_op jit(solution)/shard_map/pallas_call | solution.py:30
  88.2 4.6 %shard_map.69 = (s16[208,512]{1,0:T(8,128)(2,1)}, s16[208,512]{1,0:T(8,128)(2,1)}, s16[208,512]{1,0:T(8,128)(2,1)}, s16[208,512]{1,0:T(8,128)(2,1)}, s16[208,512...) custom-call(s32[7,6]{1,0:T(8,128)} %get-tuple-element.72.t, ...), custom_call_target="tpu_custom_call" | custom-call | tf_op jit(solution)/shard_map/pallas_call | solution.py:30
  92.8 2.3 %collective-permute-start.3 = (s16[208,512]{1,0:T(8,128)(2,1)}, s16[208,512]{1,0:T(8,128)(2,1)S(1)}, u32[]{:S(2)}, u32[]{:S(2)}) collective-permute-start(s16[208,512]{1,0:T(8,128)(2,1)} %get-tuple-element.96), channel_id=1, source_target_pairs={{0,4},{4,8},{8,12},{12,16},{16,20},{20,24},{24,28},{28,0},{1,5},{5... | collective-permute-start | bytes 638984 | tf_op jit(solution)/shard_map/ppermute | solution.py:672
  95.1 1.2 collective-permute-start.4
  96.2 1.0 collective-permute-start.6
  97.2 2.9 %collective-permute-start.7 = (s16[208,512]{1,0:T(8,128)(2,1)}, s16[208,512]{1,0:T(8,128)(2,1)S(1)}, u32[]{:S(2)}, u32[]{:S(2)}) collective-permute-start(s16[208,512]{1,0:T(8,128)(2,1)} %get-tuple-element.100), channel_id=1, source_target_pairs={{0,20},{4,24},{8,28},{12,0},{16,4},{20,8},{24,12},{28,16},{1,21},{... | collective-permute-start | bytes 638984 | tf_op jit(solution)/shard_map/ppermute | solution.py:672
  100.1 1.6 collective-permute-start.8
  101.7 5.0 %collective-permute-done.4.refs_2_ = s16[208,512]{1,0:T(8,128)(2,1)S(1)} collective-permute-done((s16[208,512]{1,0:T(8,128)(2,1)}, s16[208,512]{1,0:T(8,128)(2,1)S(1)}, u32[]{:S(2)}, u32[]{:S(2)}) %collective-permute-start.4) | collective-permute-done | bytes 213024 | tf_op jit(solution)/shard_map/ppermute | solution.py:672
  106.7 3.7 %collective-permute-done.5.refs_3_ = s16[208,512]{1,0:T(8,128)(2,1)S(1)} collective-permute-done((s16[208,512]{1,0:T(8,128)(2,1)}, s16[208,512]{1,0:T(8,128)(2,1)S(1)}, u32[]{:S(2)}, u32[]{:S(2)}) %collective-permute-start.5) | collective-permute-done | bytes 213024 | tf_op jit(solution)/shard_map/ppermute | solution.py:672
  110.4 6.3 %collective-permute-done.6.refs_4_ = s16[208,512]{1,0:T(8,128)(2,1)S(1)} collective-permute-done((s16[208,512]{1,0:T(8,128)(2,1)}, s16[208,512]{1,0:T(8,128)(2,1)S(1)}, u32[]{:S(2)}, u32[]{:S(2)}) %collective-permute-start.6) | collective-permute-done | bytes 213024 | tf_op jit(solution)/shard_map/ppermute | solution.py:672
  116.6 1.0 collective-permute-start.11
  117.7 1.8 collective-permute-start.12
  119.5 28.1 %factor.1 = (f32[512,512]{1,0:T(8,128)}, f32[512,512]{1,0:T(8,128)}) custom-call(f32[768,256]{1,0:T(8,128)} %bitcast.17), custom_call_target="tpu_custom_call" | custom-call | flops 40000000000 | bytes 2097152 | tf_op jit(solution)/shard_map/factor/pallas_call | solution.py:632
  147.7 0.7 copy-done.14
  148.3 4.5 %solve.1.x = s16[208,512]{1,0:T(8,128)(2,1)} custom-call(s32[7]{0:T(128)} %stack.31.pos, s32[24]{0:T(128)} %place.5, f32[512,512]{1,0:T(8,128)} %get-tuple-element.93.diagonal, f32[512,512]{1,0:T(8,128)} %get-tuple-element.103.inverse, s16[208,512]{1,0:T(8,128)(2,1)} %get-tuple-element.104.refs_0_, s16[208,512]{1,0:T(8,128)(2,1)} %copy-done.9, ...), custom_call_target="tpu_custom_call" | custom-call | tf_op jit(solution)/shard_map/solve/pallas_call | solution.py:747
  152.9 0.3 collective-permute-start.13
  153.2 0.3 collective-permute-start.14
  153.5 0.2 collective-permute-start.15
  153.7 0.3 collective-permute-start.16
  154.0 31.1 %shard_map.70 = (s16[8,208,512]{2,1,0:T(8,128)(2,1)}, s16[4,208,512]{2,1,0:T(8,128)(2,1)}) custom-call(s16[208,512]{1,0:T(8,128)(2,1)} %solve.1.x), custom_call_target="tpu_custom_call" | custom-call | bytes 1048576 | tf_op jit(solution)/shard_map/pallas_call | solution.py:333
  185.2 0.7 copy-done.6
  186.1 14.4 %shard_map.71 = f32[768,1536]{1,0:T(8,128)} custom-call(s32[7,18]{1,0:T(8,128)} %get-tuple-element.64.t, f32[768,1536]{1,0:T(8,128)} %front.3, s16[4,208,512]{2,1,0:T(8,128)(2,1)} %get-tuple-element.117.wr, s16[8,208,512]{2,1,0:T(8,128)(2,1)} %get-tuple-element.118.wc, s16[272,1024]{1,0:T(8,128)(2,1)} %get-tuple-element.119.refs_0_, ...), custom_call_target="tpu_custom_call" | custom-call | tf_op jit(solution)/shard_map/pallas_call | solution.py:30
  (44 shorter events, 0.4 us)
Async XLA Ops:
  7.5 64.7 %collective-permute-start = (s16[4,272,256]{2,1,0:T(8,128)(2,1)}, s16[4,272,256]{2,1,0:T(8,128)(2,1)S(1)}, u32[]{:S(2)}, u32[]{:S(2)}) collective-permute-start(s16[4,272,256]{2,1,0:T(8,128)(2,1)} %get-tuple-element.68), channel_id=1, source_target_pairs={{0,1},{1,2},{2,3},{3,0},{4,5},{5,6},{6,7},{7,4},{8,9},{9,10},{10,1... | collective-permute-start | bytes 1671176 | tf_op jit(solution)/shard_map/ppermute | solution.py:672
  7.5 64.7 %collective-permute-start.1 = (s16[4,272,256]{2,1,0:T(8,128)(2,1)}, s16[4,272,256]{2,1,0:T(8,128)(2,1)S(1)}, u32[]{:S(2)}, u32[]{:S(2)}) collective-permute-start(s16[4,272,256]{2,1,0:T(8,128)(2,1)} %get-tuple-element.69), channel_id=1, source_target_pairs={{0,2},{1,3},{2,0},{3,1},{4,6},{5,7},{6,4},{7,5},{8,10},{9,11},{10,... | collective-permute-start | bytes 1671176 | tf_op jit(solution)/shard_map/ppermute | solution.py:672
  8.8 63.4 %collective-permute-start.2 = (s16[4,272,256]{2,1,0:T(8,128)(2,1)}, s16[4,272,256]{2,1,0:T(8,128)(2,1)S(1)}, u32[]{:S(2)}, u32[]{:S(2)}) collective-permute-start(s16[4,272,256]{2,1,0:T(8,128)(2,1)} %get-tuple-element.70), channel_id=1, source_target_pairs={{0,3},{1,0},{2,1},{3,2},{4,7},{5,4},{6,5},{7,6},{8,11},{9,8},{10,9... | collective-permute-start | bytes 1671176 | tf_op jit(solution)/shard_map/ppermute | solution.py:672
  72.2 0.8 copy-start.4
  72.2 1.0 copy-start.5
  72.2 1.1 copy-start.7
  92.8 7.3 %collective-permute-start.3 = (s16[208,512]{1,0:T(8,128)(2,1)}, s16[208,512]{1,0:T(8,128)(2,1)S(1)}, u32[]{:S(2)}, u32[]{:S(2)}) collective-permute-start(s16[208,512]{1,0:T(8,128)(2,1)} %get-tuple-element.96), channel_id=1, source_target_pairs={{0,4},{4,8},{8,12},{12,16},{16,20},{20,24},{24,28},{28,0},{1,5},{5... | collective-permute-start | bytes 638984 | tf_op jit(solution)/shard_map/ppermute | solution.py:672
  95.1 11.6 %collective-permute-start.4 = (s16[208,512]{1,0:T(8,128)(2,1)}, s16[208,512]{1,0:T(8,128)(2,1)S(1)}, u32[]{:S(2)}, u32[]{:S(2)}) collective-permute-start(s16[208,512]{1,0:T(8,128)(2,1)} %get-tuple-element.97), channel_id=1, source_target_pairs={{0,8},{4,12},{8,16},{12,20},{16,24},{20,28},{24,0},{28,4},{1,9},{5... | collective-permute-start | bytes 638984 | tf_op jit(solution)/shard_map/ppermute | solution.py:672
  96.2 14.1 %collective-permute-start.5 = (s16[208,512]{1,0:T(8,128)(2,1)}, s16[208,512]{1,0:T(8,128)(2,1)S(1)}, u32[]{:S(2)}, u32[]{:S(2)}) collective-permute-start(s16[208,512]{1,0:T(8,128)(2,1)} %get-tuple-element.98), channel_id=1, source_target_pairs={{0,12},{4,16},{8,20},{12,24},{16,28},{20,0},{24,4},{28,8},{1,13},{... | collective-permute-start | bytes 638984 | tf_op jit(solution)/shard_map/ppermute | solution.py:672
  96.2 20.4 %collective-permute-start.6 = (s16[208,512]{1,0:T(8,128)(2,1)}, s16[208,512]{1,0:T(8,128)(2,1)S(1)}, u32[]{:S(2)}, u32[]{:S(2)}) collective-permute-start(s16[208,512]{1,0:T(8,128)(2,1)} %get-tuple-element.99), channel_id=1, source_target_pairs={{0,16},{4,20},{8,24},{12,28},{16,0},{20,4},{24,8},{28,12},{1,17},{... | collective-permute-start | bytes 638984 | tf_op jit(solution)/shard_map/ppermute | solution.py:672
  97.2 20.5 %collective-permute-start.7 = (s16[208,512]{1,0:T(8,128)(2,1)}, s16[208,512]{1,0:T(8,128)(2,1)S(1)}, u32[]{:S(2)}, u32[]{:S(2)}) collective-permute-start(s16[208,512]{1,0:T(8,128)(2,1)} %get-tuple-element.100), channel_id=1, source_target_pairs={{0,20},{4,24},{8,28},{12,0},{16,4},{20,8},{24,12},{28,16},{1,21},{... | collective-permute-start | bytes 638984 | tf_op jit(solution)/shard_map/ppermute | solution.py:672
  100.1 47.5 %copy-start.9 = (s16[208,512]{1,0:T(8,128)(2,1)}, s16[208,512]{1,0:T(8,128)(2,1)S(1)}, u32[]{:S(2)}) copy-start(s16[208,512]{1,0:T(8,128)(2,1)S(1)} %collective-permute-done.3.refs_1_) | copy-start | bytes 638980
  100.1 47.6 %collective-permute-start.8 = (s16[208,512]{1,0:T(8,128)(2,1)}, s16[208,512]{1,0:T(8,128)(2,1)S(1)}, u32[]{:S(2)}, u32[]{:S(2)}) collective-permute-start(s16[208,512]{1,0:T(8,128)(2,1)} %get-tuple-element.101), channel_id=1, source_target_pairs={{0,24},{4,28},{8,0},{12,4},{16,8},{20,12},{24,16},{28,20},{1,25},{... | collective-permute-start | bytes 638984 | tf_op jit(solution)/shard_map/ppermute | solution.py:672
  106.7 40.9 %copy-start.10 = (s16[208,512]{1,0:T(8,128)(2,1)}, s16[208,512]{1,0:T(8,128)(2,1)S(1)}, u32[]{:S(2)}) copy-start(s16[208,512]{1,0:T(8,128)(2,1)S(1)} %collective-permute-done.4.refs_2_) | copy-start | bytes 638980
  106.7 41.0 %collective-permute-start.9 = (s16[208,512]{1,0:T(8,128)(2,1)}, s16[208,512]{1,0:T(8,128)(2,1)}, u32[]{:S(2)}, u32[]{:S(2)}) collective-permute-start(s16[208,512]{1,0:T(8,128)(2,1)} %get-tuple-element.102), channel_id=1, source_target_pairs={{0,28},{4,0},{8,4},{12,8},{16,12},{20,16},{24,20},{28,24},{1,29},{... | collective-permute-start | bytes 638984 | tf_op jit(solution)/shard_map/ppermute | solution.py:672
  110.4 37.3 %copy-start.11 = (s16[208,512]{1,0:T(8,128)(2,1)}, s16[208,512]{1,0:T(8,128)(2,1)S(1)}, u32[]{:S(2)}) copy-start(s16[208,512]{1,0:T(8,128)(2,1)S(1)} %collective-permute-done.5.refs_3_) | copy-start | bytes 638980
  110.4 42.5 %collective-permute-start.10 = (s16[272,1024]{1,0:T(8,128)(2,1)}, s16[272,1024]{1,0:T(8,128)(2,1)S(1)}, u32[]{:S(2)}, u32[]{:S(2)}) collective-permute-start(s16[272,1024]{1,0:T(8,128)(2,1)} %get-tuple-element.113), channel_id=1, source_target_pairs={{0,8},{8,16},{16,24},{24,0},{1,9},{9,17},{17,25},{25,1},{2,10},{10... | collective-permute-start | bytes 1671176 | tf_op jit(solution)/shard_map/ppermute | solution.py:672
  116.6 31.0 %copy-start.12 = (s16[208,512]{1,0:T(8,128)(2,1)}, s16[208,512]{1,0:T(8,128)(2,1)S(1)}, u32[]{:S(2)}) copy-start(s16[208,512]{1,0:T(8,128)(2,1)S(1)} %collective-permute-done.6.refs_4_) | copy-start | bytes 638980
  116.6 36.2 %collective-permute-start.11 = (s16[272,1024]{1,0:T(8,128)(2,1)}, s16[272,1024]{1,0:T(8,128)(2,1)S(1)}, u32[]{:S(2)}, u32[]{:S(2)}) collective-permute-start(s16[272,1024]{1,0:T(8,128)(2,1)} %get-tuple-element.114), channel_id=1, source_target_pairs={{0,16},{8,24},{16,0},{24,8},{1,17},{9,25},{17,1},{25,9},{2,18},{10... | collective-permute-start | bytes 1671176 | tf_op jit(solution)/shard_map/ppermute | solution.py:672
  117.7 30.0 %copy-start.13 = (s16[208,512]{1,0:T(8,128)(2,1)}, s16[208,512]{1,0:T(8,128)(2,1)S(1)}, u32[]{:S(2)}) copy-start(s16[208,512]{1,0:T(8,128)(2,1)S(1)} %collective-permute-done.7.refs_5_) | copy-start | bytes 638980
  117.7 35.2 %collective-permute-start.12 = (s16[272,1024]{1,0:T(8,128)(2,1)}, s16[272,1024]{1,0:T(8,128)(2,1)S(1)}, u32[]{:S(2)}, u32[]{:S(2)}) collective-permute-start(s16[272,1024]{1,0:T(8,128)(2,1)} %get-tuple-element.115), channel_id=1, source_target_pairs={{0,24},{8,0},{16,8},{24,16},{1,25},{9,1},{17,9},{25,17},{2,26},{10... | collective-permute-start | bytes 1671176 | tf_op jit(solution)/shard_map/ppermute | solution.py:672
  147.6 5.3 %copy-start = (s16[272,1024]{1,0:T(8,128)(2,1)S(1)}, s16[272,1024]{1,0:T(8,128)(2,1)}, u32[]{:S(2)}) copy-start(s16[272,1024]{1,0:T(8,128)(2,1)} %get-tuple-element.119.refs_0_) | copy-start | bytes 1671172
  147.7 0.7 copy-start.14
  152.9 32.3 %copy-start.1 = (s16[272,1024]{1,0:T(8,128)(2,1)}, s16[272,1024]{1,0:T(8,128)(2,1)S(1)}, u32[]{:S(2)}) copy-start(s16[272,1024]{1,0:T(8,128)(2,1)S(1)} %collective-permute-done.10.refs_1_) | copy-start | bytes 1671172
  152.9 32.3 %copy-start.2 = (s16[272,1024]{1,0:T(8,128)(2,1)}, s16[272,1024]{1,0:T(8,128)(2,1)S(1)}, u32[]{:S(2)}) copy-start(s16[272,1024]{1,0:T(8,128)(2,1)S(1)} %collective-permute-done.11.refs_2_) | copy-start | bytes 1671172
  152.9 32.3 %copy-start.3 = (s16[272,1024]{1,0:T(8,128)(2,1)}, s16[272,1024]{1,0:T(8,128)(2,1)S(1)}, u32[]{:S(2)}) copy-start(s16[272,1024]{1,0:T(8,128)(2,1)S(1)} %collective-permute-done.12.refs_3_) | copy-start | bytes 1671172
  152.9 32.2 %collective-permute-start.13 = (s16[272,1024]{1,0:T(8,128)(2,1)S(1)}, s16[272,1024]{1,0:T(8,128)(2,1)S(1)}, u32[]{:S(2)}, u32[]{:S(2)}) collective-permute-start(s16[272,1024]{1,0:T(8,128)(2,1)S(1)} %copy-done), channel_id=1, source_target_pairs={{0,4},{4,0},{1,5},{5,1},{2,6},{6,2},{3,7},{7,3},{8,12},{12,8},{9,1... | collective-permute-start | bytes 1671176 | tf_op jit(solution)/shard_map/ppermute | solution.py:672
  153.2 31.9 %collective-permute-start.14 = (s16[272,1024]{1,0:T(8,128)(2,1)S(1)}, s16[272,1024]{1,0:T(8,128)(2,1)S(1)}, u32[]{:S(2)}, u32[]{:S(2)}) collective-permute-start(s16[272,1024]{1,0:T(8,128)(2,1)S(1)} %collective-permute-done.10.refs_1_), channel_id=1, source_target_pairs={{0,4},{4,0},{1,5},{5,1},{2,6},{6,2},{3,7},{7,3},{8,12},{12,8},{9,1... | collective-permute-start | bytes 1671176 | tf_op jit(solution)/shard_map/ppermute | solution.py:672
  153.5 31.6 %collective-permute-start.15 = (s16[272,1024]{1,0:T(8,128)(2,1)S(1)}, s16[272,1024]{1,0:T(8,128)(2,1)}, u32[]{:S(2)}, u32[]{:S(2)}) collective-permute-start(s16[272,1024]{1,0:T(8,128)(2,1)S(1)} %collective-permute-done.11.refs_2_), channel_id=1, source_target_pairs={{0,4},{4,0},{1,5},{5,1},{2,6},{6,2},{3,7},{7,3},{8,12},{12,8},{9,1... | collective-permute-start | bytes 1671176 | tf_op jit(solution)/shard_map/ppermute | solution.py:672
  153.7 31.4 %collective-permute-start.16 = (s16[272,1024]{1,0:T(8,128)(2,1)S(1)}, s16[272,1024]{1,0:T(8,128)(2,1)}, u32[]{:S(2)}, u32[]{:S(2)}) collective-permute-start(s16[272,1024]{1,0:T(8,128)(2,1)S(1)} %collective-permute-done.12.refs_3_), channel_id=1, source_target_pairs={{0,4},{4,0},{1,5},{5,1},{2,6},{6,2},{3,7},{7,3},{8,12},{12,8},{9,1... | collective-permute-start | bytes 1671176 | tf_op jit(solution)/shard_map/ppermute | solution.py:672
  185.1 0.8 copy-start.6
  185.1 1.0 copy-start.8
